TPU v7x, 32 devices: a whole 2x2x4 slice. The times are simulated.
32 devices in a mesh: dp: 8 (over z, y), mp: 4 (over x, core).
Axes of the slice: x: 2, y: 2, z: 4, core: 2. Of those that a mesh axis runs over, the one named last changes fastest.
Arguments:
- tokens: bfloat16 [8, 2048, 768], P('dp', 'mp'), may hold values from -6 to 6
- picture_ids: int32 [8, 2048], P('dp'), may hold values from -1 to 10, as said below
- w_qkv: bfloat16 [768, 3, 768], P('dp', None, 'mp'), may hold values from -0.21875 to 0.21875
- w_out: bfloat16 [768, 768], P('dp', 'mp'), may hold values from -3.5 to 3.5
- w_up: bfloat16 [768, 3072], P('dp', 'mp'), may hold values from -0.21875 to 0.21875
- w_down: bfloat16 [768, 3072], P('dp', 'mp'), may hold values from -0.109375 to 0.109375
- ln1_gain: float32 [768], P(('dp', 'mp')), may hold values from 0.5 to 1.5
- ln1_bias: float32 [768], P(('dp', 'mp')), may hold values from -3 to 3
- q_gain: float32 [768], P(('dp', 'mp')), may hold values from 0.5 to 2
- k_gain: float32 [768], P(('dp', 'mp')), may hold values from 0.5 to 2
- out_bias: float32 [768], P(('dp', 'mp')), may hold values from -3 to 3
- ln2_gain: float32 [768], P(('dp', 'mp')), may hold values from 0.5 to 1.5
- ln2_bias: float32 [768], P(('dp', 'mp')), may hold values from -3 to 3
- up_bias: float32 [3072], P(('dp', 'mp')), may hold values from -3 to 3
- down_bias: float32 [768], P(('dp', 'mp')), may hold values from -3 to 3
- cotangent: bfloat16 [8, 2048, 768], P('dp', 'mp'), may hold values from -6 to 6
Outputs:
- output: bfloat16 [8, 2048, 768], P('dp', 'mp')
- tokens_grad: bfloat16 [8, 2048, 768], P('dp', 'mp')
- w_qkv_grad: float32 [768, 3, 768], P('dp', None, 'mp')
- w_out_grad: float32 [768, 768], P('dp', 'mp')
- w_up_grad: float32 [768, 3072], P('dp', 'mp')
- w_down_grad: float32 [768, 3072], P('dp', 'mp')
- ln1_gain_grad: float32 [768], P(('dp', 'mp'))
- ln1_bias_grad: float32 [768], P(('dp', 'mp'))
- q_gain_grad: float32 [768], P(('dp', 'mp'))
- k_gain_grad: float32 [768], P(('dp', 'mp'))
- out_bias_grad: float32 [768], P(('dp', 'mp'))
- ln2_gain_grad: float32 [768], P(('dp', 'mp'))
- ln2_bias_grad: float32 [768], P(('dp', 'mp'))
- up_bias_grad: float32 [3072], P(('dp', 'mp'))
- down_bias_grad: float32 [768], P(('dp', 'mp'))
Inputs may be any that keep to these rules, and one draw needn't show every extreme that they name: `picture_ids`: in each row the positions form consecutive pictures numbered 0, 1, 2, ... from the start, each of 100 to 1024 positions, and one of the first two pictures has exactly 1024; the positions after the last whole picture are padding, marked -1. Some row holds the largest number of pictures that fits.
All inputs are finite; a program needn't handle non-finite values.
Results may differ from a plain program's by a relative error of at most 0.019.
Values may be sent and summed in bfloat16 or wider, within the bound.
A program may use at most 128 MiB of HBM per device.

v0:
```python
import jax
import jax.numpy as jnp
from jax import lax
from jax.sharding import PartitionSpec as P

HEAD_DIM = 64
QBLOCK = 512


EPSILON = 1e-06


def layer_norm(values, scaling, shifts):
    centre = jnp.mean(values, axis=-1, keepdims=True)
    centred = values - centre
    spread = jnp.mean(centred * centred, axis=-1, keepdims=True)
    return centred * lax.rsqrt(spread + EPSILON) * scaling + shifts


def head_norm(values, scaling):
    centre = jnp.mean(values, axis=-1, keepdims=True)
    centred = values - centre
    spread = jnp.mean(centred * centred, axis=-1, keepdims=True)
    return centred * lax.rsqrt(spread + EPSILON) * scaling


def gelu_exact(values):
    return jax.nn.gelu(values, approximate=False)


def permitted(label_rows, label_cols, place_rows, place_cols):
    same_pic = (label_rows[:, None] == label_cols[None, :]) & (label_rows[:, None] >= 0)
    return same_pic | (place_rows[:, None] == place_cols[None, :])


def attend_row(query_rows, key_rows, value_rows, labels):
    length, heads_here = (query_rows.shape[0], query_rows.shape[1])
    blocks = length // QBLOCK
    scaling = HEAD_DIM ** (-0.5)
    places = jnp.arange(length, dtype=jnp.int32)

    def one_block(inputs):
        query_block, label_block, place_block = inputs
        scores = (
            jnp.einsum("qhd,khd->hqk", query_block, key_rows, preferred_element_type=jnp.float32)
            * scaling
        )
        allowed = permitted(label_block, labels, place_block, places)
        scores = jnp.where(allowed[None], scores, -1e30)
        summit = jnp.max(scores, axis=-1, keepdims=True)
        weights_exp = jnp.exp(scores - summit)
        totals = jnp.sum(weights_exp, axis=-1, keepdims=True)
        chances = (weights_exp / totals).astype(jnp.bfloat16)
        mixed = jnp.einsum("hqk,khd->qhd", chances, value_rows, preferred_element_type=jnp.float32)
        return (mixed.astype(jnp.bfloat16), (summit + jnp.log(totals))[..., 0])

    mixed, summits = lax.map(
        one_block,
        (
            query_rows.reshape(blocks, QBLOCK, heads_here, HEAD_DIM),
            labels.reshape(blocks, QBLOCK),
            places.reshape(blocks, QBLOCK),
        ),
    )
    return (mixed.reshape(length, heads_here, HEAD_DIM), summits)


def attend_back(query_rows, key_rows, value_rows, labels, summits, grad_rows):
    length, heads_here = (query_rows.shape[0], query_rows.shape[1])
    blocks = length // QBLOCK
    scaling = HEAD_DIM ** (-0.5)
    places = jnp.arange(length, dtype=jnp.int32)

    def one_block(carried, inputs):
        key_grad, value_grad = carried
        query_block, label_block, place_block, summit_block, grad_block = inputs
        scores = (
            jnp.einsum("qhd,khd->hqk", query_block, key_rows, preferred_element_type=jnp.float32)
            * scaling
        )
        allowed = permitted(label_block, labels, place_block, places)
        chances = jnp.where(allowed[None], jnp.exp(scores - summit_block[..., None]), 0.0)
        chance_low = chances.astype(jnp.bfloat16)
        value_grad = value_grad + jnp.einsum(
            "hqk,qhd->khd", chance_low, grad_block, preferred_element_type=jnp.float32
        )
        weighed = jnp.einsum(
            "qhd,khd->hqk", grad_block, value_rows, preferred_element_type=jnp.float32
        )
        centre = jnp.sum(chances * weighed, axis=-1, keepdims=True)
        score_grad = (chances * (weighed - centre)).astype(jnp.bfloat16)
        query_grad = (
            jnp.einsum("hqk,khd->qhd", score_grad, key_rows, preferred_element_type=jnp.float32)
            * scaling
        )
        key_grad = (
            key_grad
            + jnp.einsum(
                "hqk,qhd->khd", score_grad, query_block, preferred_element_type=jnp.float32
            )
            * scaling
        )
        return ((key_grad, value_grad), query_grad)

    zero_rows = jnp.zeros((length, heads_here, HEAD_DIM), jnp.float32)
    inputs = (
        query_rows.reshape(blocks, QBLOCK, heads_here, HEAD_DIM),
        labels.reshape(blocks, QBLOCK),
        places.reshape(blocks, QBLOCK),
        summits,
        grad_rows.reshape(blocks, QBLOCK, heads_here, HEAD_DIM),
    )
    (key_grad, value_grad), query_grad = lax.scan(one_block, (zero_rows, zero_rows), inputs)
    return (query_grad.reshape(length, heads_here, HEAD_DIM), key_grad, value_grad)


def body(
    tokens,
    picture_ids,
    w_qkv,
    w_out,
    w_up,
    w_down,
    ln1_gain,
    ln1_bias,
    q_gain,
    k_gain,
    out_bias,
    ln2_gain,
    ln2_bias,
    up_bias,
    down_bias,
    cotangent,
):
    qkv_full, out_full, up_full, down_full = (
        lax.all_gather(w_qkv, "dp", axis=0, tiled=True),
        lax.all_gather(w_out, "dp", axis=0, tiled=True),
        lax.all_gather(w_up, "dp", axis=0, tiled=True),
        lax.all_gather(w_down, "dp", axis=0, tiled=True),
    )
    (
        gain_one,
        shift_one,
        q_scale_all,
        k_scale_all,
        bias_out,
        gain_two,
        shift_two,
        up_shift_all,
        bias_down,
    ) = (
        lax.all_gather(ln1_gain, ("dp", "mp"), axis=0, tiled=True),
        lax.all_gather(ln1_bias, ("dp", "mp"), axis=0, tiled=True),
        lax.all_gather(q_gain, ("dp", "mp"), axis=0, tiled=True),
        lax.all_gather(k_gain, ("dp", "mp"), axis=0, tiled=True),
        lax.all_gather(out_bias, ("dp", "mp"), axis=0, tiled=True),
        lax.all_gather(ln2_gain, ("dp", "mp"), axis=0, tiled=True),
        lax.all_gather(ln2_bias, ("dp", "mp"), axis=0, tiled=True),
        lax.all_gather(up_bias, ("dp", "mp"), axis=0, tiled=True),
        lax.all_gather(down_bias, ("dp", "mp"), axis=0, tiled=True),
    )
    head_cols = w_qkv.shape[2]
    heads_here = head_cols // HEAD_DIM
    unit_cols = w_up.shape[1]
    mp_rank = lax.axis_index("mp")
    q_scale = lax.dynamic_slice_in_dim(q_scale_all, mp_rank * head_cols, head_cols).reshape(
        heads_here, HEAD_DIM
    )
    k_scale = lax.dynamic_slice_in_dim(k_scale_all, mp_rank * head_cols, head_cols).reshape(
        heads_here, HEAD_DIM
    )
    tokens_f32 = tokens.astype(jnp.float32)
    normed = layer_norm(tokens_f32, gain_one, shift_one).astype(jnp.bfloat16)
    normed_rows = lax.all_gather(normed, "mp", axis=1, tiled=True)
    projected = jnp.einsum(
        "rtd,dce->rtce", normed_rows, qkv_full, preferred_element_type=jnp.float32
    )
    row_count, length = (projected.shape[0], projected.shape[1])
    query_raw = projected[:, :, 0].reshape(row_count, length, heads_here, HEAD_DIM)
    key_raw = projected[:, :, 1].reshape(row_count, length, heads_here, HEAD_DIM)
    value_low = (
        projected[:, :, 2].reshape(row_count, length, heads_here, HEAD_DIM).astype(jnp.bfloat16)
    )
    query_low = head_norm(query_raw, q_scale).astype(jnp.bfloat16)
    key_low = head_norm(key_raw, k_scale).astype(jnp.bfloat16)
    attended, summits = lax.map(
        lambda inputs: attend_row(inputs[0], inputs[1], inputs[2], inputs[3]),
        (query_low, key_low, value_low, picture_ids),
    )
    attended = attended.reshape(row_count, length, head_cols)
    branch = lax.psum_scatter(
        jnp.einsum("rte,de->rtd", attended, out_full, preferred_element_type=jnp.float32).astype(
            jnp.bfloat16
        ),
        "mp",
        scatter_dimension=1,
        tiled=True,
    ).astype(jnp.float32)
    middle = tokens_f32 + branch + bias_out
    normed_two = layer_norm(middle, gain_two, shift_two).astype(jnp.bfloat16)
    up_shift = lax.dynamic_slice_in_dim(up_shift_all, mp_rank * unit_cols, unit_cols)
    normed_two_rows = lax.all_gather(normed_two, "mp", axis=1, tiled=True)
    up_pre = (
        jnp.einsum("rtd,df->rtf", normed_two_rows, up_full, preferred_element_type=jnp.float32)
        + up_shift
    )
    activated, gelu_pull = jax.vjp(gelu_exact, up_pre)
    activated_low = activated.astype(jnp.bfloat16)
    mlp_out = lax.psum_scatter(
        jnp.einsum(
            "rtf,df->rtd", activated_low, down_full, preferred_element_type=jnp.float32
        ).astype(jnp.bfloat16),
        "mp",
        scatter_dimension=1,
        tiled=True,
    ).astype(jnp.float32)
    result = middle + mlp_out + bias_down
    grad_y = cotangent.astype(jnp.float32)
    grad_down_bias = jnp.sum(grad_y, axis=(0, 1))
    grad_rows = lax.all_gather(cotangent, "mp", axis=1, tiled=True)
    grad_act = jnp.einsum("rtd,df->rtf", grad_rows, down_full, preferred_element_type=jnp.float32)
    grad_down_w = jnp.einsum(
        "rtd,rtf->df", grad_rows, activated_low, preferred_element_type=jnp.float32
    )
    grad_pre_low = gelu_pull(grad_act)[0].astype(jnp.bfloat16)
    grad_up_w = jnp.einsum(
        "rtd,rtf->df", normed_two_rows, grad_pre_low, preferred_element_type=jnp.float32
    )
    grad_up_here = jnp.sum(grad_pre_low, axis=(0, 1), dtype=jnp.float32)
    grad_up_bias = lax.dynamic_update_slice_in_dim(
        jnp.zeros(up_shift_all.shape, jnp.float32), grad_up_here, mp_rank * unit_cols, 0
    )
    grad_normed_two = lax.psum_scatter(
        jnp.einsum("rtf,df->rtd", grad_pre_low, up_full, preferred_element_type=jnp.float32).astype(
            jnp.bfloat16
        ),
        "mp",
        scatter_dimension=1,
        tiled=True,
    ).astype(jnp.float32)
    _, norm_two_pull = jax.vjp(layer_norm, middle, gain_two, shift_two)
    grad_mid_part, grad_gain_two, grad_shift_two = norm_two_pull(grad_normed_two)
    grad_middle = grad_y + grad_mid_part
    grad_out_bias = jnp.sum(grad_middle, axis=(0, 1))
    grad_mid_rows = lax.all_gather(grad_middle.astype(jnp.bfloat16), "mp", axis=1, tiled=True)
    grad_out_w = jnp.einsum(
        "rtd,rte->de", grad_mid_rows, attended, preferred_element_type=jnp.float32
    )
    grad_attended = jnp.einsum(
        "rtd,de->rte", grad_mid_rows, out_full, preferred_element_type=jnp.float32
    ).astype(jnp.bfloat16)
    grad_attended = grad_attended.reshape(row_count, length, heads_here, HEAD_DIM)
    query_grad, key_grad, value_grad = lax.map(
        lambda inputs: attend_back(
            inputs[0], inputs[1], inputs[2], inputs[3], inputs[4], inputs[5]
        ),
        (query_low, key_low, value_low, picture_ids, summits, grad_attended),
    )
    _, query_pull = jax.vjp(head_norm, query_raw, q_scale)
    grad_query_raw, grad_q_scale = query_pull(query_grad)
    _, key_pull = jax.vjp(head_norm, key_raw, k_scale)
    grad_key_raw, grad_k_scale = key_pull(key_grad)
    grad_projected = (
        jnp.stack([grad_query_raw, grad_key_raw, value_grad], axis=2)
        .reshape(row_count, length, 3, head_cols)
        .astype(jnp.bfloat16)
    )
    grad_qkv_w = jnp.einsum(
        "rtd,rtce->dce", normed_rows, grad_projected, preferred_element_type=jnp.float32
    )
    grad_normed = lax.psum_scatter(
        jnp.einsum(
            "rtce,dce->rtd", grad_projected, qkv_full, preferred_element_type=jnp.float32
        ).astype(jnp.bfloat16),
        "mp",
        scatter_dimension=1,
        tiled=True,
    ).astype(jnp.float32)
    _, norm_one_pull = jax.vjp(layer_norm, tokens_f32, gain_one, shift_one)
    grad_x_part, grad_gain_one, grad_shift_one = norm_one_pull(grad_normed)
    grad_tokens = (grad_middle + grad_x_part).astype(jnp.bfloat16)
    grad_q_all = lax.dynamic_update_slice_in_dim(
        jnp.zeros(q_scale_all.shape, jnp.float32),
        grad_q_scale.reshape(head_cols),
        mp_rank * head_cols,
        0,
    )
    grad_k_all = lax.dynamic_update_slice_in_dim(
        jnp.zeros(k_scale_all.shape, jnp.float32),
        grad_k_scale.reshape(head_cols),
        mp_rank * head_cols,
        0,
    )
    weight_parts = (
        lax.psum_scatter(grad_qkv_w, "dp", scatter_dimension=0, tiled=True),
        lax.psum_scatter(grad_out_w, "dp", scatter_dimension=0, tiled=True),
        lax.psum_scatter(grad_up_w, "dp", scatter_dimension=0, tiled=True),
        lax.psum_scatter(grad_down_w, "dp", scatter_dimension=0, tiled=True),
    )
    vector_parts = (
        lax.psum_scatter(grad_gain_one, ("dp", "mp"), scatter_dimension=0, tiled=True),
        lax.psum_scatter(grad_shift_one, ("dp", "mp"), scatter_dimension=0, tiled=True),
        lax.psum_scatter(grad_q_all, ("dp", "mp"), scatter_dimension=0, tiled=True),
        lax.psum_scatter(grad_k_all, ("dp", "mp"), scatter_dimension=0, tiled=True),
        lax.psum_scatter(grad_out_bias, ("dp", "mp"), scatter_dimension=0, tiled=True),
        lax.psum_scatter(grad_gain_two, ("dp", "mp"), scatter_dimension=0, tiled=True),
        lax.psum_scatter(grad_shift_two, ("dp", "mp"), scatter_dimension=0, tiled=True),
        lax.psum_scatter(grad_up_bias, ("dp", "mp"), scatter_dimension=0, tiled=True),
        lax.psum_scatter(grad_down_bias, ("dp", "mp"), scatter_dimension=0, tiled=True),
    )
    return (
        result.astype(jnp.bfloat16),
        grad_tokens,
        weight_parts[0],
        weight_parts[1],
        weight_parts[2],
        weight_parts[3],
        vector_parts[0],
        vector_parts[1],
        vector_parts[2],
        vector_parts[3],
        vector_parts[4],
        vector_parts[5],
        vector_parts[6],
        vector_parts[7],
        vector_parts[8],
    )


def solution(mesh):
    return jax.shard_map(
        body,
        mesh=mesh,
        in_specs=(
            P("dp", "mp", None),
            P("dp", None),
            P("dp", None, "mp"),
            P("dp", "mp"),
            P("dp", "mp"),
            P("dp", "mp"),
            P(("dp", "mp")),
            P(("dp", "mp")),
            P(("dp", "mp")),
            P(("dp", "mp")),
            P(("dp", "mp")),
            P(("dp", "mp")),
            P(("dp", "mp")),
            P(("dp", "mp")),
            P(("dp", "mp")),
            P("dp", "mp", None),
        ),
        out_specs=(
            P("dp", "mp", None),
            P("dp", "mp", None),
            P("dp", None, "mp"),
            P("dp", "mp"),
            P("dp", "mp"),
            P("dp", "mp"),
            P(("dp", "mp")),
            P(("dp", "mp")),
            P(("dp", "mp")),
            P(("dp", "mp")),
            P(("dp", "mp")),
            P(("dp", "mp")),
            P(("dp", "mp")),
            P(("dp", "mp")),
            P(("dp", "mp")),
        ),
        check_vma=False,
    )
```

profile of v0, /device:TPU:0, one launch (start us, length us, event | category | flops | bytes accessed | tf_op | source)
XLA Modules:
  0.0 1012.6 jit_solution(15082478609487470339)
XLA Ops:
  13.1 42.9 %all-reduce.19 = (f32[768]{0:T(1024)}, f32[768]{0:T(1024)}, f32[768]{0:T(1024)S(1)}, f32[768]{0:T(1024)S(1)}, f32[768]{0:T(1024)S(1)}, /*index=5*/f32[768]{0:T(1024)S(1)}, f32[768]{0:T(1024)}, f32[3072]{0:T(1024)}) all-reduce(f32[768]{0:T(1024)S(1)} %dynamic-update-slice.6, ...), channel_id=1, replica_groups=mesh['dp'=8,'mp'=4] {'dp','mp'}, use_global_device_ids=true, to_apply=%add.6 | all-reduce | flops 8448 | bytes 67584
  60.2 37.2 %all_gather.54 = bf16[768,3,192]{2,1,0:T(4,128)(2,1)S(1)} all-gather(bf16[96,3,192]{2,1,0:T(4,128)(2,1)S(1)} %copy.78), channel_id=1, replica_groups=mesh['dp'=8,'mp'=4] {'dp'}, dimensions={0}, use_global_device_ids=true | all-gather | bytes 995328 | tf_op jit(solution)/shard_map/all_gather | solution.py:136
  99.0 31.2 %all_gather.57 = bf16[768,192]{1,0:T(8,128)(2,1)S(1)} all-gather(bf16[96,192]{1,0:T(8,128)(2,1)S(1)} %copy-done.63), channel_id=1, replica_groups=mesh['dp'=8,'mp'=4] {'dp'}, dimensions={0}, use_global_device_ids=true | all-gather | bytes 331776 | tf_op jit(solution)/shard_map/all_gather | solution.py:137
  146.8 91.3 %while.48 = (s32[]{:T(128)}, bf16[4,512,3,64]{1,3,2,0:T(8,128)(2,1)}, f32[4,3,512]{2,1,0:T(4,128)}, s32[4,512]{1,0:T(4,128)S(1)}, s32[2048]{0:T(1024)S(1)}, /*in...) while((s32[]{:T(128)}, ...), condition=%wide.region_9.10_spmd.clone, body=%wide.region_6.9_spmd.clone.sunk | while | flops 847346688 | bytes 43983996 | solution.py:57
  149.0 5.9 fusion.161
  155.0 6.8 fusion.162
  161.8 7.3 fusion.163
  171.9 5.9 fusion.161
  177.8 6.8 fusion.162
  184.6 7.3 fusion.163
  194.7 5.9 fusion.161
  200.6 6.8 fusion.162
  207.4 7.3 fusion.163
  217.5 5.9 fusion.161
  223.4 6.8 fusion.162
  230.2 7.3 fusion.163
  245.0 36.3 %reduce-scatter.11.cloned.1.call-done = bf16[1,512,768]{2,1,0:T(8,128)(2,1)} async-done(((bf16[1,2048,768]{2,1,0:T(8,128)(2,1)}), bf16[1,512,768]{2,1,0:T(8,128)(2,1)}) %reduce-scatter.11.cloned.1.call-update) | async-done | bytes 786448 | tf_op jit(solution)/shard_map/reduce_scatter | solution.py:191
  288.6 27.7 %all-gather.9.cloned.1.call-done = bf16[1,2048,768]{2,1,0:T(8,128)(2,1)} async-done(((bf16[1,512,768]{2,1,0:T(8,128)(2,1)}), bf16[1,2048,768]{2,1,0:T(8,128)(2,1)}) %all-gather.9.cloned.1.call-update) | async-done | bytes 3145744 | tf_op jit(solution)/shard_map/all_gather | solution.py:202
  316.4 19.0 %multiply_convert_fusion.1 = (bf16[2048,768]{1,0:T(8,128)(2,1)}, f32[2048,768]{1,0:T(8,128)}, f32[2048,768]{1,0:T(8,128)}) fusion(f32[768]{0:T(1024)} %dynamic_slice.61, bf16[768,768]{1,0:T(8,128)(2,1)} %all-gather.11.cloned.1.call-done, bf16[1,2048,768]{2,1,0:T(8,128)(2,1)} %all-gather.9.cloned.1.call-done), kind=kOutput, calls=%fused_computation.64 | convolution fusion | flops 2519728128 | bytes 20057088 | tf_op jit(solution)/shard_map/rtd,df->rtf/dot_general | solution.py:204
  335.4 24.9 %all-gather.13.cloned.1.call-done = bf16[768,768]{1,0:T(8,128)(2,1)} async-done(((bf16[96,768]{1,0:T(8,128)(2,1)}), bf16[768,768]{1,0:T(8,128)(2,1)}) %all-gather.13.cloned.1.call-update) | async-done | bytes 1179664 | tf_op jit(solution)/shard_map/all_gather | solution.py:139
  360.2 28.5 %all-gather.15.cloned.1.call-done = bf16[1,2048,768]{2,1,0:T(8,128)(2,1)} async-done(((bf16[1,512,768]{2,1,0:T(8,128)(2,1)}), bf16[1,2048,768]{2,1,0:T(8,128)(2,1)}) %all-gather.15.cloned.1.call-update) | async-done | bytes 3145744 | tf_op jit(solution)/shard_map/all_gather | solution.py:220
  388.8 11.1 %convert_reduce_fusion = (f32[768]{0:T(1024)}, bf16[2048,768]{1,0:T(8,128)(2,1)S(1)}) fusion(f32[2048,768]{1,0:T(8,128)} %get-tuple-element.464, bf16[768,768]{1,0:T(8,128)(2,1)} %all-gather.13.cloned.1.call-done, bf16[1,2048,768]{2,1,0:T(8,128)(2,1)} %all-gather.15.cloned.1.call-done, f32[2048,768]{1,0:T(8,128)} %get-tuple-element.480, f32[768]{0:T(1024)} %dynamic_slice.61), kind=kOutput, calls=%fused_computation.62 | convolution fusion | flops 2442657024 | bytes 20060160 | tf_op jit(solution)/shard_map/rtd,df->rtf/dot_general | solution.py:221
  405.7 38.1 %reduce-scatter.15.cloned.1.call-done = bf16[1,512,768]{2,1,0:T(8,128)(2,1)} async-done(((bf16[1,2048,768]{2,1,0:T(8,128)(2,1)}), bf16[1,512,768]{2,1,0:T(8,128)(2,1)}) %reduce-scatter.15.cloned.1.call-update) | async-done | bytes 786448 | tf_op jit(solution)/shard_map/reduce_scatter | solution.py:233
  453.1 28.4 %all-gather.17.cloned.1.call-done = bf16[1,2048,768]{2,1,0:T(8,128)(2,1)} async-done(((bf16[1,512,768]{2,1,0:T(8,128)(2,1)}), bf16[1,2048,768]{2,1,0:T(8,128)(2,1)}) %all-gather.17.cloned.1.call-update) | async-done | bytes 3145744 | tf_op jit(solution)/shard_map/all_gather | solution.py:245
  485.3 132.8 %while.49 = (s32[]{:T(128)}, f32[2048,3,64]{0,2,1:T(8,128)}, f32[2048,3,64]{0,2,1:T(8,128)}, f32[4,512,3,64]{1,3,2,0:T(8,128)}, bf16[4,512,3,64]{1,3,2,0:T(8,128...) while((s32[]{:T(128)}, f32[2048,3,64]{0,2,1:T(8,128)}, ...), condition=%wide.region_19.20_spmd.clone, body=%wide.region_17.19_spmd.clone.sunk | while | flops 2066709504 | bytes 169283040 | solution.py:113
  495.7 5.8 multiply_reduce_fusion.9
  501.4 4.9 multiply_convert_fusion.5
  511.4 6.2 fusion.177
  523.6 5.5 fusion.176
  529.1 5.8 multiply_reduce_fusion.9
  534.9 4.9 multiply_convert_fusion.5
  544.9 6.2 fusion.177
  557.1 5.5 fusion.176
  562.6 5.8 multiply_reduce_fusion.9
  568.4 4.9 multiply_convert_fusion.5
  578.3 6.1 fusion.177
  590.5 5.5 fusion.176
  596.0 5.8 multiply_reduce_fusion.9
  611.8 6.2 fusion.177
  644.8 6.2 fusion.71
  651.1 6.2 fusion.87
  659.4 7.6 fusion.64
  670.4 6.6 fusion.54
  685.6 40.5 %all-reduce.18 = (f32[768]{0:T(1024)S(1)}, f32[768]{0:T(1024)S(1)}, f32[768]{0:T(1024)S(1)}, f32[768]{0:T(1024)S(1)}, f32[768]{0:T(1024)S(1)}, /*index=5*/f32[76...) all-reduce(f32[768]{0:T(1024)S(1)} %dynamic-update-slice.8, ...), channel_id=1, replica_groups=mesh['dp'=8,'mp'=4] {'dp','mp'}, use_global_device_ids=true, to_apply=%add.8 | all-reduce | flops 9984 | bytes 79872
  734.6 60.7 %reduce-scatter.25.cloned.1.call-done = f32[96,768]{1,0:T(8,128)} async-done(((f32[768,768]{1,0:T(8,128)}), f32[96,768]{1,0:T(8,128)}) %reduce-scatter.25.cloned.1.call-update) | async-done | bytes 294928
  795.4 72.0 %reduce-scatter.23.cloned.1.call-done = f32[96,768]{1,0:T(8,128)} async-done(((f32[768,768]{1,0:T(8,128)}), f32[96,768]{1,0:T(8,128)}) %reduce-scatter.23.cloned.1.call-update) | async-done | bytes 294928 | tf_op jit(solution)/shard_map/reduce_scatter | solution.py:297
  867.4 65.3 %reduce-scatter.21.cloned.1.call-done = f32[96,192]{1,0:T(8,128)} async-done(((f32[768,192]{1,0:T(8,128)}), f32[96,192]{1,0:T(8,128)}) %reduce-scatter.21.cloned.1.call-update) | async-done | bytes 73744 | tf_op jit(solution)/shard_map/reduce_scatter | solution.py:296
  932.7 72.4 %reduce-scatter.19.cloned.1.call-done = f32[96,3,192]{2,0,1:T(8,128)} async-done(((f32[768,3,192]{2,0,1:T(8,128)}), f32[96,3,192]{2,0,1:T(8,128)}) %reduce-scatter.19.cloned.1.call-update) | async-done | bytes 221200 | tf_op jit(solution)/shard_map/reduce_scatter | solution.py:295
  (439 shorter events, 173.0 us)
Async XLA Ops:
  8.0 48.0 %copy-start.4 = (bf16[1,512,768]{2,1,0:T(8,128)(2,1)S(1)}, bf16[1,512,768]{2,1,0:T(8,128)(2,1)}, u32[]{:S(2)}) copy-start(bf16[1,512,768]{2,1,0:T(8,128)(2,1)} %param.20) | copy-start | bytes 2359300
  8.1 122.0 %all-gather.7.cloned.1.call-start = ((), (), s32[]{:S(2)}) async-start(), calls=%async_computation.8 | async-start | bytes 3932160 | tf_op jit(solution)/shard_map/all_gather | solution.py:174
  9.5 47.7 %copy-start.56 = (f32[512]{0:T(512)}, f32[512]{0:T(512)S(1)}, u32[]{:S(2)}) copy-start(f32[512]{0:T(512)S(1)} %broadcast_multiply_fusion.3) | copy-start | bytes 6148
  9.6 48.3 %copy-start.37 = (s32[1,2048]{1,0:T(1,128)S(1)}, s32[1,2048]{1,0:T(1,128)}, u32[]{:S(2)}) copy-start(s32[1,2048]{1,0:T(1,128)} %param.21) | copy-start | bytes 24580
  9.6 50.5 %copy-start.54 = (bf16[96,3,192]{2,0,1:T(8,128)(2,1)S(1)}, bf16[96,3,192]{2,0,1:T(8,128)(2,1)}, u32[]{:S(2)}) copy-start(bf16[96,3,192]{2,0,1:T(8,128)(2,1)} %param.22) | copy-start | bytes 331780
  11.1 48.9 %copy-start.64 = (f32[512]{0:T(512)}, f32[512]{0:T(512)S(1)}, u32[]{:S(2)}) copy-start(f32[512]{0:T(512)S(1)} %fusion.108) | copy-start | bytes 6148
  57.3 224.0 %reduce-scatter.11.cloned.1.call-start = ((), (), s32[]{:S(2)}) async-start(), calls=%async_computation.9 | async-start | bytes 3932160 | tf_op jit(solution)/shard_map/reduce_scatter | solution.py:191
  98.3 35.7 %copy-start.38 = (bf16[768,3,192]{0,2,1:T(8,128)(2,1)}, bf16[768,3,192]{0,2,1:T(8,128)(2,1)S(1)}, u32[]{:S(2)}) copy-start(bf16[768,3,192]{0,2,1:T(8,128)(2,1)S(1)} %copy.79) | copy-start | bytes 2654212
  136.7 7.8 copy-start.10
  244.0 37.4 %copy-start.5 = (bf16[1,512,768]{2,1,0:T(8,128)(2,1)S(1)}, bf16[1,512,768]{2,1,0:T(8,128)(2,1)}, u32[]{:S(2)}) copy-start(bf16[1,512,768]{2,1,0:T(8,128)(2,1)} %param.20) | copy-start | bytes 2359300
  244.0 37.4 %copy-start.52 = (f32[768]{0:T(1024)S(1)}, f32[768]{0:T(1024)}, u32[]{:S(2)}) copy-start(f32[768]{0:T(1024)} %get-tuple-element.459) | copy-start | bytes 9220
  244.0 44.7 %all-gather.11.cloned.1.call-start = ((), (), s32[]{:S(2)}) async-start(), calls=%async_computation.11 | async-start | bytes 1327104 | tf_op jit(solution)/shard_map/all_gather | solution.py:138
  244.6 71.8 %all-gather.9.cloned.1.call-start = ((), (), s32[]{:S(2)}) async-start(), calls=%async_computation.10 | async-start | bytes 3932160 | tf_op jit(solution)/shard_map/all_gather | solution.py:202
  285.9 74.3 %all-gather.13.cloned.1.call-start = ((), (), s32[]{:S(2)}) async-start(), calls=%async_computation.12 | async-start | bytes 1327104 | tf_op jit(solution)/shard_map/all_gather | solution.py:139
  286.5 102.3 %all-gather.15.cloned.1.call-start = ((), (), s32[]{:S(2)}) async-start(), calls=%async_computation.14 | async-start | bytes 3932160 | tf_op jit(solution)/shard_map/all_gather | solution.py:220
  287.2 156.5 %reduce-scatter.15.cloned.1.call-start = ((), (), s32[]{:S(2)}) async-start(), calls=%async_computation.15 | async-start | bytes 3932160 | tf_op jit(solution)/shard_map/reduce_scatter | solution.py:233
  388.8 12.8 %copy-start.81 = (bf16[768,768]{1,0:T(8,128)(2,1)S(1)}, bf16[768,768]{1,0:T(8,128)(2,1)}, u32[]{:S(2)}) copy-start(bf16[768,768]{1,0:T(8,128)(2,1)} %all-gather.11.cloned.1.call-done) | copy-start | bytes 3538948
  405.6 75.9 %all-gather.17.cloned.1.call-start = ((), (), s32[]{:S(2)}) async-start(), calls=%async_computation.16 | async-start | bytes 3932160 | tf_op jit(solution)/shard_map/all_gather | solution.py:245
  453.0 228.7 %reduce-scatter.17.cloned.1.call-start = ((), (), s32[]{:S(2)}) async-start(), calls=%async_computation.17 | async-start | bytes 3932160 | tf_op jit(solution)/shard_map/reduce_scatter | solution.py:271
  501.4 7.5 copy-start.7
  511.4 6.2 copy-start.8
  511.4 6.2 copy-start.13
  511.4 6.2 copy-start.28
  534.9 7.5 copy-start.7
  544.8 6.2 copy-start.8
  544.9 6.2 copy-start.13
  568.4 7.5 copy-start.7
  601.8 7.5 copy-start.7
  611.7 6.2 copy-start.8
  611.7 6.2 copy-start.13
  611.8 6.2 copy-start.28
  628.8 9.8 copy-start.41
  631.6 7.0 copy-start.40
  643.6 87.7 %reduce-scatter.13.cloned.1.call-start = ((), (), s32[]{:S(2)}) async-start(), calls=%async_computation.13 | async-start | bytes 3932160 | tf_op jit(solution)/shard_map/reduce_scatter | solution.py:209
  651.0 144.3 %reduce-scatter.25.cloned.1.call-start = ((), (), s32[]{:S(2)}) async-start(), calls=%async_computation.21 | async-start | bytes 2654208
  659.4 208.0 %reduce-scatter.23.cloned.1.call-start = ((), (), s32[]{:S(2)}) async-start(), calls=%async_computation.20 | async-start | bytes 2654208 | tf_op jit(solution)/shard_map/reduce_scatter | solution.py:297
  659.4 7.7 copy-start.30
  667.0 265.6 %reduce-scatter.21.cloned.1.call-start = ((), (), s32[]{:S(2)}) async-start(), calls=%async_computation.19 | async-start | bytes 884736 | tf_op jit(solution)/shard_map/reduce_scatter | solution.py:296
  670.2 334.9 %reduce-scatter.19.cloned.1.call-start = ((), (), s32[]{:S(2)}) async-start(), calls=%async_computation.18 | async-start | bytes 2654208 | tf_op jit(solution)/shard_map/reduce_scatter | solution.py:295
  677.0 6.4 copy-start.70
  677.0 6.4 copy-start.65
  678.7 6.8 copy-start.72
  678.7 6.8 copy-start.73
  678.7 6.8 copy-start.74
  678.7 6.9 copy-start.75
  678.7 52.6 %copy-start.17 = (bf16[1,512,768]{2,1,0:T(8,128)(2,1)S(1)}, bf16[1,512,768]{2,1,0:T(8,128)(2,1)}, u32[]{:S(2)}) copy-start(bf16[1,512,768]{2,1,0:T(8,128)(2,1)} %reduce-scatter.11.cloned.1.call-done) | copy-start | bytes 2359300
  678.7 52.6 %copy-start.21 = (f32[1,512,768]{2,1,0:T(8,128)S(1)}, f32[1,512,768]{2,1,0:T(8,128)}, u32[]{:S(2)}) copy-start(f32[1,512,768]{2,1,0:T(8,128)} %copy-done.20) | copy-start | bytes 4718596
  678.7 52.6 %copy-start.53 = (f32[768]{0:T(1024)S(1)}, f32[768]{0:T(1024)}, u32[]{:S(2)}) copy-start(f32[768]{0:T(1024)} %get-tuple-element.459) | copy-start | bytes 9220
  (88 other events, 264.8 us)
Sparse Core Ops, SparseCore 0:
  57.4 28.6 all-gather.6
  244.1 37.1 reduce-scatter.10
  405.7 37.9 reduce-scatter.14
  643.7 37.9 reduce-scatter.16
  684.3 38.1 reduce-scatter.12
  726.4 68.9 reduce-scatter.24
  799.5 67.8 reduce-scatter.22
  871.2 61.3 reduce-scatter.20
  937.2 67.8 reduce-scatter.18
Sparse Core Ops, SparseCore 1:
  246.9 40.5 all-gather.10
  289.5 26.8 all-gather.8
  318.7 41.5 all-gather.12
  361.9 26.8 all-gather.14
  453.1 28.3 all-gather.16
where the time goes:
time: 1020 us; the launch traced here: 1010 us
  waiting for transfers between devices  459 us (45%)
  matrix products  220 us (22%)
  blocking collectives  152 us (15%)
  other arithmetic  99 us (10%)
  local copies, waits for them, and re-layouts  62.7 us (6%)
  between operations  16.8 us (2%)
    unnamed x2, blocking collectives  83.4 us
    reduce_scatter x1, waiting for transfers between devices, body(): lax.psum_scatter(grad_qkv_w, 'dp', scatter_dimension=0, tiled=True)  72.4 us
    reduce_scatter x1, waiting for transfers between devices, body(): lax.psum_scatter(grad_up_w, 'dp', scatter_dimension=0, tiled=True)  72 us
    reduce_scatter x1, waiting for transfers between devices, body(): lax.psum_scatter(grad_out_w, 'dp', scatter_dimension=0, tiled=True)  65.3 us
    unnamed x15, waiting for transfers between devices  62.6 us
    reduce_scatter x1, waiting for transfers between devices, body(): lax.psum_scatter(jnp.einsum('rtf,df->rtd', grad_pre_low, up_full, preferr...  38.1 us
    all_gather x1, blocking collectives, body(): lax.all_gather(w_qkv, 'dp', axis=0, tiled=True)  37.2 us
    reduce_scatter x1, waiting for transfers between devices, body(): lax.psum_scatter(jnp.einsum('rte,de->rtd', attended, out_full, preferred_...  36.3 us
  transfers between devices with their start and end apart: 14, of which 11 were waited for; matrix products, arithmetic and copies ran while one was open for 7% of the time, Pallas kernels for 0%

commit v1 on v0

v1 whole, which is shorter than its diff:
```python
import functools

import jax
import jax.numpy as jnp
from jax import lax
from jax.experimental import pallas as pl
from jax.experimental.pallas import tpu as pltpu
from jax.sharding import PartitionSpec as P

F32 = jnp.float32
BF = jnp.bfloat16
HEAD = 64
EPS = 1e-06
TB = 256
BIG = 32768.0
LOG2E = 1.4426950408889634
MESH = pl.DeviceIdType.MESH
ANY = pl.BlockSpec(memory_space=pl.ANY)
VM = pl.BlockSpec(memory_space=pltpu.VMEM)
SM = pl.BlockSpec(memory_space=pltpu.SMEM)
VLIM = 60 * 1024 * 1024


def nn(a, b):
    return lax.dot_general(a, b, (((1,), (0,)), ((), ())), preferred_element_type=F32)


def nt(a, b):
    return lax.dot_general(a, b, (((1,), (1,)), ((), ())), preferred_element_type=F32)


def tn(a, b):
    return lax.dot_general(a, b, (((0,), (0,)), ((), ())), preferred_element_type=F32)


def sds(shape, dtype):
    return jax.ShapeDtypeStruct(shape, dtype)


def params(**kw):
    return pltpu.CompilerParams(vmem_limit_bytes=VLIM, **kw)


def cost(flops, nbytes, trans=0):
    return pl.CostEstimate(flops=int(flops), bytes_accessed=int(nbytes), transcendentals=int(trans))


def rcopy(src, dst, ssem, rsem, peer):
    return pltpu.make_async_remote_copy(
        src_ref=src,
        dst_ref=dst,
        send_sem=ssem,
        recv_sem=rsem,
        device_id=peer,
        device_id_type=MESH,
    )


def greet(peers):
    bar = pltpu.get_barrier_semaphore()
    for p in peers:
        pl.semaphore_signal(bar, inc=1, device_id=p, device_id_type=MESH)
    pl.semaphore_wait(bar, len(peers))


def gather_kernel(
    nz, nc, tok, w, vec, tok_all, w_all, vec_all, loc, zs, zr, ys, yr, xs, xr, cs, cr, tx, rx, tc, rc
):
    dp, mp = lax.axis_index("dp"), lax.axis_index("mp")
    z, y, x, c = dp // 2, dp % 2, mp // 2, mp % 2
    xm, cm, dm = (1 - x) * 2 + c, x * 2 + 1 - c, (1 - x) * 2 + 1 - c
    ypeer, xpeer, cpeer = (z * 2 + 1 - y, mp), (dp, xm), (dp, cm)
    zpeers = [(((z + k) % nz) * 2 + y, mp) for k in range(1, nz)]
    greet(zpeers + [ypeer, xpeer, cpeer])
    rows = tok.shape[0] // nc
    xt = []
    for i in range(nc):
        part = pl.ds(i * rows, rows)
        cp = rcopy(tok.at[part], tok_all.at[mp, part], tx.at[i], rx.at[i], xpeer)
        cp.start()
        xt.append(cp)
    zc = []
    for k in range(1, nz):
        for kind, (src, dst) in enumerate(((vec, vec_all.at[mp, dp]), (w, w_all.at[dp]))):
            cp = rcopy(src, dst, zs.at[kind, k], zr.at[kind, k], zpeers[k - 1])
            cp.start()
            zc.append(cp)
    yc = []
    for kind, (src, dst) in enumerate(((vec, vec_all.at[mp, dp]), (w, w_all.at[dp]))):
        cp = rcopy(src, dst, ys.at[kind, 0], yr.at[kind, 0], ypeer)
        cp.start()
        yc.append(cp)
    own_tok = rcopy(tok, tok_all.at[mp], tc.at[nc], rc.at[nc], cpeer)
    own_tok.start()
    locs = [
        pltpu.make_async_copy(tok, tok_all.at[mp], loc.at[0]),
        pltpu.make_async_copy(w, w_all.at[dp], loc.at[1]),
        pltpu.make_async_copy(vec, vec_all.at[mp, dp], loc.at[2]),
    ]
    for cp in locs:
        cp.start()
    for k in range(1, nz):
        src_dp = ((z + nz - k) % nz) * 2 + y
        for kind in range(2):
            zc[(k - 1) * 2 + kind].wait_recv()
            ref = (vec_all.at[mp, src_dp], w_all.at[src_dp])[kind]
            cp = rcopy(ref, ref, ys.at[kind, k], yr.at[kind, k], ypeer)
            cp.start()
            yc.append(cp)
    ct = []

    def forward(i):
        part = pl.ds(i * rows, rows)
        xt[i].wait_recv()
        cp = rcopy(tok_all.at[xm, part], tok_all.at[xm, part], tc.at[i], rc.at[i], cpeer)
        cp.start()
        ct.append(cp)

    forward(0)
    for cp in locs:
        cp.wait()
    for k in range(nz):
        yc[k * 2].wait_recv()
    vx = rcopy(vec_all.at[mp], vec_all.at[mp], xs, xr, xpeer)
    vx.start()
    vc0 = rcopy(vec_all.at[mp], vec_all.at[mp], cs.at[0], cr.at[0], cpeer)
    vc0.start()
    if nc > 1:
        forward(1)
    vx.wait_recv()
    vc1 = rcopy(vec_all.at[xm], vec_all.at[xm], cs.at[1], cr.at[1], cpeer)
    vc1.start()
    for i in range(2, nc):
        forward(i)
    for k in range(nz):
        yc[k * 2 + 1].wait_recv()
    for cp in ct:
        cp.wait_recv()
    own_tok.wait()
    vc0.wait()
    vc1.wait()
    vx.wait_send()
    for cp in zc + yc + xt + ct:
        cp.wait_send()


def gather_all(tok, w, vec, ndp, nmp):
    nz, nc = ndp // 2, 4
    dma = pltpu.SemaphoreType.DMA
    return pl.pallas_call(
        functools.partial(gather_kernel, nz, nc),
        out_shape=(
            sds((nmp,) + tok.shape, BF),
            sds((ndp,) + w.shape, BF),
            sds((nmp, ndp) + vec.shape, F32),
        ),
        in_specs=[ANY] * 3,
        out_specs=(ANY,) * 3,
        scratch_shapes=[
            dma((3,)),
            dma((2, nz)),
            dma((2, nz)),
            dma((2, nz)),
            dma((2, nz)),
            dma,
            dma,
            dma((2,)),
            dma((2,)),
            dma((nc,)),
            dma((nc,)),
            dma((nc + 1,)),
            dma((nc + 1,)),
        ],
        compiler_params=pltpu.CompilerParams(collective_id=0, has_side_effects=True),
        name="gather_start",
    )(tok, w, vec)


def swap_kernel(forward, nmp, src, dst, loc, ss, rs):
    dp, mp = lax.axis_index("dp"), lax.axis_index("mp")
    own = dst.shape[2] if forward else src.shape[2]
    peers = [(mp + k) % nmp for k in range(1, nmp)]
    greet([(dp, m) for m in peers])

    def ends(m):
        if forward:
            return src.at[:, pl.ds(pl.multiple_of(m * own, own), own)], dst.at[mp]
        return src.at[m], dst.at[:, pl.ds(pl.multiple_of(mp * own, own), own)]

    cps = []
    for k, m in enumerate(peers):
        s, d = ends(m)
        cp = rcopy(s, d, ss.at[k], rs.at[k], (dp, m))
        cp.start()
        cps.append(cp)
    s, d = ends(mp)
    lc = pltpu.make_async_copy(s, d, loc)
    lc.start()
    lc.wait()
    for cp in cps:
        cp.wait()


def swap(src, forward, nmp, cid):
    dma = pltpu.SemaphoreType.DMA
    if forward:
        shape = (nmp, src.shape[0], src.shape[1] // nmp)
    else:
        shape = (src.shape[1], src.shape[2] * nmp)
    return pl.pallas_call(
        functools.partial(swap_kernel, forward, nmp),
        out_shape=sds(shape, BF),
        in_specs=[ANY],
        out_specs=ANY,
        scratch_shapes=[dma, dma((nmp - 1,)), dma((nmp - 1,))],
        compiler_params=pltpu.CompilerParams(collective_id=cid, has_side_effects=True),
        name="swap_fwd" if forward else "swap_bwd",
    )(src)


def vector_kernel(ndp, nmp, src, out, got, ss, rs):
    dp, mp = lax.axis_index("dp"), lax.axis_index("mp")
    me, n = dp * nmp + mp, ndp * nmp
    peers = [(me + k) % n for k in range(1, n)]
    greet([(p // nmp, p % nmp) for p in peers])
    cps = []
    for k, p in enumerate(peers):
        cp = rcopy(src.at[p], got.at[k], ss.at[k], rs.at[k], (p // nmp, p % nmp))
        cp.start()
        cps.append(cp)
    total = src[me]
    for k, cp in enumerate(cps):
        cp.wait_recv()
        total = total + got[k]
    out[...] = total
    for cp in cps:
        cp.wait_send()


def vector_sums(parts, ndp, nmp):
    n = ndp * nmp
    dma = pltpu.SemaphoreType.DMA
    return pl.pallas_call(
        functools.partial(vector_kernel, ndp, nmp),
        out_shape=sds(parts.shape[1:], F32),
        in_specs=[VM],
        out_specs=VM,
        scratch_shapes=[pltpu.VMEM((n - 1,) + parts.shape[1:], F32), dma((n - 1,)), dma((n - 1,))],
        compiler_params=pltpu.CompilerParams(collective_id=3, has_side_effects=True),
        name="vector_sums",
    )(parts)


def norm_rows(v):
    centre = jnp.mean(v, axis=-1, keepdims=True)
    v = v - centre
    r = lax.rsqrt(jnp.mean(v * v, axis=-1, keepdims=True) + EPS)
    return v * r, r


def norm_cols(v):
    centre = jnp.mean(v, axis=0, keepdims=True)
    v = v - centre
    r = lax.rsqrt(jnp.mean(v * v, axis=0, keepdims=True) + EPS)
    return v * r, r


def qkv_kernel(heads, tok, w, gain, shift, gains, normed, raw, low, wt):
    @pl.when(pl.program_id(0) == 0)
    def _():
        wt[...] = w[...].T

    cols = heads * HEAD
    hat, _ = norm_rows(tok[0].astype(F32))
    n = (hat * gain[...] + shift[...]).astype(BF)
    normed[...] = n
    proj = nt(wt[0 : 3 * cols, :], n)
    raw[...] = proj[0 : 2 * cols]
    for h in range(2 * heads):
        part = slice(h * HEAD, (h + 1) * HEAD)
        hat, _ = norm_cols(proj[part])
        low[part, :] = (hat * gains[part, :]).astype(BF)
    low[2 * cols :, :] = proj[2 * cols :].astype(BF)


def project(tok_all, w, gain, shift, gains, heads):
    nb, rows, d = tok_all.shape
    cols = heads * HEAD
    t = nb * rows
    full = lambda shape: pl.BlockSpec(shape, lambda i: (0,) * len(shape))
    return pl.pallas_call(
        functools.partial(qkv_kernel, heads),
        grid=(nb,),
        out_shape=(
            sds((t, d), BF),
            sds((2 * cols, t), F32),
            sds((3 * cols, t), BF),
            sds((w.shape[1], w.shape[0]), BF),
        ),
        in_specs=[
            pl.BlockSpec((1, rows, d), lambda i: (i, 0, 0)),
            full(w.shape),
            full((1, d)),
            full((1, d)),
            full((2 * cols, 1)),
        ],
        out_specs=(
            pl.BlockSpec((rows, d), lambda i: (i, 0)),
            pl.BlockSpec((2 * cols, rows), lambda i: (0, i)),
            pl.BlockSpec((3 * cols, rows), lambda i: (0, i)),
            full((w.shape[1], w.shape[0])),
        ),
        compiler_params=params(),
        cost_estimate=cost(2 * t * d * 3 * cols, 12 * 2**20),
        name="project_qkv",
    )(tok_all, w, gain, shift, gains)


def masks(ids):
    t = ids.shape[1]
    r = lax.broadcasted_iota(jnp.int32, (2 * HEAD, t), 0)
    pad = ids < 0
    mq = jnp.where(r == ids, 1.0, 0.0)
    mq = jnp.where((r == 31) & pad, 1.0, mq)
    mk = jnp.where((r < 31) & (r != ids), -BIG, 0.0)
    mk = jnp.where(r == 31, -BIG, mk)
    mk = jnp.where((r >= 32) & (r < 35), 1.0, mk)
    return mq, mk


def three(v):
    a = v.astype(BF).astype(F32)
    b = (v - a).astype(BF).astype(F32)
    return a, b, v - a - b


def split_query(q):
    s = q.astype(F32) * (LOG2E * HEAD**-0.5)
    hi = s.astype(BF)
    return hi, (s - hi.astype(F32)).astype(BF)


def attend_kernel(heads, nblk, span, low, ids, out, lse, qa, ka, va, acc):
    cols = heads * HEAD
    t = ids.shape[1]
    mq, mk = masks(ids[...])
    mq, mkt = mq.astype(BF), mk.T.astype(BF)
    one = jnp.where(lax.broadcasted_iota(jnp.int32, (16, t), 0) == 0, 1.0, 0.0).astype(BF)
    for h in range(heads):
        hi, lo = split_query(low[h * HEAD : (h + 1) * HEAD, :])
        qa[h, 0:HEAD, :] = hi
        qa[h, HEAD : 2 * HEAD, :] = lo
        qa[h, 2 * HEAD :, :] = mq
        k = low[cols + h * HEAD : cols + (h + 1) * HEAD, :].astype(F32)
        ka[h, :, 0 : 2 * HEAD] = jnp.concatenate([k, k], axis=0).T.astype(BF)
        ka[h, :, 2 * HEAD :] = mkt
        va[h, 0:HEAD, :] = low[2 * cols + h * HEAD : 2 * cols + (h + 1) * HEAD, :]
        va[h, HEAD:, :] = one
    acc[...] = jnp.zeros_like(acc)

    def row(i, _):
        qi = pl.ds(pl.multiple_of(i * TB, TB), TB)

        def col(j, _):
            kj = pl.ds(pl.multiple_of(j * TB, TB), TB)
            for h in range(heads):
                s = nn(ka[h, kj, :], qa[h, :, qi])
                acc[h, :, qi] += nn(va[h, :, kj], jnp.exp2(s).astype(BF))
            return 0

        return lax.fori_loop(span[i], span[nblk + i], col, 0)

    lax.fori_loop(0, nblk, row, 0)
    pad = ids[...] < 0
    lse[...] = jnp.zeros_like(lse)
    for h in range(heads):
        total = jnp.where(pad, 1.0, acc[h, HEAD : HEAD + 1, :])
        value = low[2 * cols + h * HEAD : 2 * cols + (h + 1) * HEAD, :].astype(F32)
        o = jnp.where(pad, value, acc[h, 0:HEAD, :] / total)
        out[h * HEAD : (h + 1) * HEAD, :] = o.astype(BF)
        lse[h : h + 1, :] = jnp.log2(total)


def attend(span, low, ids, heads):
    cols, t = heads * HEAD, low.shape[1]
    return pl.pallas_call(
        functools.partial(attend_kernel, heads, t // TB),
        out_shape=(sds((cols, t), BF), sds((8, t), F32)),
        in_specs=[SM, VM, VM],
        out_specs=(VM, VM),
        scratch_shapes=[
            pltpu.VMEM((heads, 4 * HEAD, t), BF),
            pltpu.VMEM((heads, t, 4 * HEAD), BF),
            pltpu.VMEM((heads, HEAD + 16, t), BF),
            pltpu.VMEM((heads, HEAD + 16, t), F32),
        ],
        compiler_params=params(),
        cost_estimate=cost(12e9, 4 * 2**20),
        name="attend",
    )(span, low, ids)


def head_back(raw, gain, grad):
    hat, r = norm_cols(raw)
    e = grad * gain
    m1 = jnp.mean(e, axis=0, keepdims=True)
    m2 = jnp.mean(e * hat, axis=0, keepdims=True)
    return (e - m1 - hat * m2) * r, jnp.sum(grad * hat, axis=1, keepdims=True)


def attend_back_kernel(
    heads, nblk, span, low, raw, att, lse, dout, ids, gains, gproj, ggain, qa, ka, va, da, dq, dk, dv
):
    cols = heads * HEAD
    t = ids.shape[1]
    mq, mk = masks(ids[...])
    mkt = mk.T.astype(BF)
    r = lax.broadcasted_iota(jnp.int32, (2 * HEAD, t), 0)
    r64 = lax.broadcasted_iota(jnp.int32, (HEAD, t), 0)
    one = jnp.where(r64 < 3, 1.0, 0.0)
    for h in range(heads):
        hs = slice(h * HEAD, (h + 1) * HEAD)
        hi, lo = split_query(low[hs, :])
        qa[h, 0:HEAD, :] = hi
        qa[h, HEAD : 2 * HEAD, :] = lo
        a, b, c = three(-lse[h : h + 1, :])
        m = jnp.where(r == 32, a, jnp.where(r == 33, b, jnp.where(r == 34, c, mq)))
        qa[h, 2 * HEAD :, :] = m.astype(BF)
        k = low[cols + h * HEAD : cols + (h + 1) * HEAD, :].astype(F32)
        ka[h, :, 0 : 2 * HEAD] = jnp.concatenate([k, k], axis=0).T.astype(BF)
        ka[h, :, 2 * HEAD :] = mkt
        v = low[2 * cols + h * HEAD : 2 * cols + (h + 1) * HEAD, :].astype(F32)
        va[h, :, :] = jnp.concatenate([v, one], axis=0).T.astype(BF)
        do = dout[hs, :]
        delta = jnp.sum(do.astype(F32) * att[hs, :].astype(F32), axis=0, keepdims=True)
        a, b, c = three(-delta)
        da[h, 0:HEAD, :] = do
        da[h, HEAD:, :] = jnp.where(
            r64 == 0, a, jnp.where(r64 == 1, b, jnp.where(r64 == 2, c, 0.0))
        ).astype(BF)
    dq[...] = jnp.zeros_like(dq)
    dk[...] = jnp.zeros_like(dk)
    dv[...] = jnp.zeros_like(dv)

    def row(i, _):
        qi = pl.ds(pl.multiple_of(i * TB, TB), TB)

        def col(j, _):
            kj = pl.ds(pl.multiple_of(j * TB, TB), TB)
            for h in range(heads):
                hs = pl.ds(h * HEAD, HEAD)
                p = jnp.exp2(nn(ka[h, kj, :], qa[h, :, qi]))
                ds = (p * nn(va[h, kj, :], da[h, :, qi])).astype(BF)
                dv[hs, kj] += nt(dout[hs, qi], p.astype(BF))
                dk[hs, kj] += nt(low[hs, qi], ds)
                dq[hs, qi] += nn(low[pl.ds(cols + h * HEAD, HEAD), kj], ds)
            return 0

        return lax.fori_loop(span[i], span[nblk + i], col, 0)

    lax.fori_loop(0, nblk, row, 0)
    pad = ids[...] < 0
    scale = HEAD**-0.5
    for h in range(heads):
        hs = slice(h * HEAD, (h + 1) * HEAD)
        for part, grad in ((0, dq), (1, dk)):
            ps = slice(part * cols + h * HEAD, part * cols + (h + 1) * HEAD)
            g, gg = head_back(raw[ps, :], gains[ps, :], grad[hs, :] * scale)
            gproj[ps, :] = g.astype(BF)
            ggain[ps, :] = gg
        g = dv[hs, :] + jnp.where(pad, dout[hs, :].astype(F32), 0.0)
        gproj[2 * cols + h * HEAD : 2 * cols + (h + 1) * HEAD, :] = g.astype(BF)


def attend_back(span, low, raw, att, lse, dout, ids, gains, heads):
    cols, t = heads * HEAD, low.shape[1]
    return pl.pallas_call(
        functools.partial(attend_back_kernel, heads, t // TB),
        out_shape=(sds((3 * cols, t), BF), sds((2 * cols, 1), F32)),
        in_specs=[SM] + [VM] * 7,
        out_specs=(VM, VM),
        scratch_shapes=[
            pltpu.VMEM((heads, 4 * HEAD, t), BF),
            pltpu.VMEM((heads, t, 4 * HEAD), BF),
            pltpu.VMEM((heads, t, 2 * HEAD), BF),
            pltpu.VMEM((heads, 2 * HEAD, t), BF),
            pltpu.VMEM((cols, t), F32),
            pltpu.VMEM((cols, t), F32),
            pltpu.VMEM((cols, t), F32),
        ],
        compiler_params=params(),
        cost_estimate=cost(30e9, 12 * 2**20),
        name="attend_back",
    )(span, low, raw, att, lse, dout, ids, gains)


def place_out(pieces, dest):
    mp = lax.axis_index("mp")
    x, c = mp // 2, mp % 2
    order = (mp, (1 - x) * 2 + c, x * 2 + 1 - c, (1 - x) * 2 + 1 - c)
    rows = pieces[0].shape[0]
    for piece, m in zip(pieces, order):
        dest[pl.ds(pl.multiple_of(m * rows, rows), rows), :] = piece[...]


def middle_kernel(att, w0, w1, w2, w3, tok, bias, gain, shift, mid, low, wo):
    place_out((w0, w1, w2, w3), wo)
    m = tok[...].astype(F32) + tn(att[...], wo[...]) + bias[...]
    mid[...] = m
    hat, _ = norm_rows(m)
    low[...] = (hat * gain[...] + shift[...]).astype(BF)


def middle_part(att, wos, tok, bias, gain, shift):
    rows, d = tok.shape
    return pl.pallas_call(
        middle_kernel,
        out_shape=(sds((rows, d), F32), sds((rows, d), BF)),
        in_specs=[VM] * 9,
        out_specs=(VM, VM),
        scratch_shapes=[pltpu.VMEM((d, d), BF)],
        compiler_params=params(),
        cost_estimate=cost(2 * rows * d * d, 6 * 2**20),
        name="middle",
    )(att, *wos, tok, bias, gain, shift)


def middle_back_kernel(
    nmp, g0, g1, mid, cot, att, w0, w1, w2, w3, gain, gmid, gatt, gwo, sums, wo
):
    place_out((w0, w1, w2, w3), wo)
    gy = cot[...].astype(F32)
    g = g0[...] + g1[...].astype(F32)
    hat, r = norm_rows(mid[...])
    e = g * gain[...]
    m1 = jnp.mean(e, axis=-1, keepdims=True)
    m2 = jnp.mean(e * hat, axis=-1, keepdims=True)
    gm = gy + (e - m1 - hat * m2) * r
    gmid[...] = gm
    low = gm.astype(BF)
    rows = att.shape[0] // nmp
    ga = nt(wo[...], low).astype(BF)
    for m in range(nmp):
        gatt[m] = ga[m * rows : (m + 1) * rows]
    gw = nt(gm.T.astype(BF), att[...]).astype(BF)
    mp = lax.axis_index("mp")
    for m in range(nmp):
        gwo[m] = gw[:, m * rows : (m + 1) * rows]
    sums[...] = jnp.zeros_like(sums)
    for k, v in enumerate((gm, g * hat, g, gy)):
        sums[k : k + 1, :] = jnp.sum(v, axis=0, keepdims=True)


def middle_back(g0, g1, mid, cot, att, wos, gain, nmp):
    rows, d = mid.shape
    return pl.pallas_call(
        functools.partial(middle_back_kernel, nmp),
        out_shape=(
            sds((rows, d), F32),
            sds((nmp, d // nmp, rows), BF),
            sds((nmp, d, d // nmp), BF),
            sds((8, d), F32),
        ),
        in_specs=[VM] * 10,
        out_specs=(VM,) * 4,
        scratch_shapes=[pltpu.VMEM((d, d), BF)],
        compiler_params=params(),
        cost_estimate=cost(4 * rows * d * d, 10 * 2**20),
        name="middle_back",
    )(g0, g1, mid, cot, att, *wos, gain)


def feed_kernel(npiece, nz, *refs):
    n0, n1, c0, c1, bias = refs[:5]
    pieces = refs[5 : 5 + npiece]
    out_own, out_send, g_own, g_send, dwu, dwd, gbias = refs[5 + npiece : 12 + npiece]
    wu, wd, n2, gy, n2t, gyt, acts, gps, oacc, gacc, sem = refs[12 + npiece :]
    dp, mp = lax.axis_index("dp"), lax.axis_index("mp")
    z, y, x, c = dp // 2, dp % 2, mp // 2, mp % 2
    copies = []
    half = npiece // 2
    for a, piece in enumerate(pieces):
        dest = (wu, wd)[a // half]
        rel = a % half
        count, rows = piece.shape[0], piece.shape[1]
        for k in range(count):
            if half == 2:
                at, colidx = 0, rel
            else:
                zz = (z + nz - k) % nz
                at = (zz * 2 + (y if rel % 2 == 0 else 1 - y)) * rows
                at, colidx = pl.multiple_of(at, rows), rel // 2
            cp = pltpu.make_async_copy(piece.at[k], dest.at[colidx, pl.ds(at, rows), :], sem.at[a, k])
            cp.start()
            copies.append(cp)
    hr = n0.shape[0]
    for i, (n, g) in enumerate(((n0, c0), (n1, c1))):
        part = slice(i * hr, (i + 1) * hr)
        n2[part, :] = n[...]
        gy[part, :] = g[...]
        n2t[:, part] = n[...].T
        gyt[:, part] = g[...].T
    oacc[...] = jnp.zeros_like(oacc)
    gacc[...] = jnp.zeros_like(gacc)
    for cp in copies:
        cp.wait()
    rows, d = n2.shape
    cw = acts.shape[1]
    per = wu.shape[2] // cw
    ones = jnp.ones((16, rows), BF)

    def chunk(i, _):
        col, off = i // per, pl.multiple_of((i % per) * cw, cw)
        cs = pl.ds(off, cw)
        m = jnp.where(col == 0, mp, (1 - x) * 2 + c)
        b = bias[pl.ds(m, 1), cs]
        for rb in range(rows // 256):
            rs = slice(rb * 256, (rb + 1) * 256)
            u = nn(n2[rs, :], wu[col, :, cs]) + b
            ga = nn(gy[rs, :], wd[col, :, cs])
            cdf = 0.5 + 0.5 * lax.erf(u * 0.7071067811865476)
            act = (u * cdf).astype(BF)
            gp = (ga * (cdf + u * (jnp.exp(-0.5 * u * u) * 0.3989422804014327))).astype(BF)
            acts[rs, :] = act
            gps[rs, :] = gp
            oacc[rs, :] += nt(act, wd[col, :, cs])
            gacc[rs, :] += nt(gp, wu[col, :, cs])
        dwd[col, :, cs] = nn(gyt[...], acts[...]).astype(BF)
        dwu[col, :, cs] = nn(n2t[...], gps[...]).astype(BF)
        gbias[col, :, cs] = nn(ones, gps[...])[0:8]
        return 0

    lax.fori_loop(0, 2 * per, chunk, 0)
    out_own[...] = oacc[0:hr]
    out_send[...] = oacc[hr:].astype(BF)
    g_own[...] = gacc[0:hr]
    g_send[...] = gacc[hr:].astype(BF)


def feed(n0, n1, c0, c1, bias, ups, downs, nz):
    hr, d = n0.shape
    rows, cw = 2 * hr, 256
    unit = ups[0].shape[2]
    pieces = list(ups) + list(downs)
    kmax = max(p.shape[0] for p in pieces)
    vm = pltpu.VMEM
    return pl.pallas_call(
        functools.partial(feed_kernel, len(pieces), nz),
        out_shape=(
            sds((hr, d), F32),
            sds((hr, d), BF),
            sds((hr, d), F32),
            sds((hr, d), BF),
            sds((2, d, unit), BF),
            sds((2, d, unit), BF),
            sds((2, 8, unit), F32),
        ),
        in_specs=[VM] * 5 + [ANY] * len(pieces),
        out_specs=(VM,) * 7,
        scratch_shapes=[
            vm((2, d, unit), BF),
            vm((2, d, unit), BF),
            vm((rows, d), BF),
            vm((rows, d), BF),
            vm((d, rows), BF),
            vm((d, rows), BF),
            vm((rows, cw), BF),
            vm((rows, cw), BF),
            vm((rows, d), F32),
            vm((rows, d), F32),
            pltpu.SemaphoreType.DMA((len(pieces), kmax)),
        ],
        compiler_params=params(),
        cost_estimate=cost(12 * rows * d * 2 * unit, 22 * 2**20),
        name="feed_forward",
    )(n0, n1, c0, c1, bias, *pieces)


def project_back_kernel(order, gproj, normed, tok, wt, gn, gw, sums, acc):
    @pl.when(pl.program_id(0) == 0)
    def _():
        acc[...] = jnp.zeros_like(acc)
        sums[...] = jnp.zeros_like(sums)

    acc[...] += nn(gproj[...], normed[...])
    g = tn(gproj[...], wt[...])
    gn[0] = g.astype(BF)
    hat, _ = norm_rows(tok[0].astype(F32))
    sums[0:1, :] += jnp.sum(g * hat, axis=0, keepdims=True)
    sums[1:2, :] += jnp.sum(g, axis=0, keepdims=True)

    @pl.when(pl.program_id(0) == pl.num_programs(0) - 1)
    def _():
        gw[...] = acc[...].T.astype(BF)


def project_back(order, gproj, normed, tok_all, wt):
    nb, rows, d = tok_all.shape
    n = gproj.shape[0]
    t = nb * rows
    return pl.pallas_call(
        project_back_kernel,
        grid_spec=pltpu.PrefetchScalarGridSpec(
            num_scalar_prefetch=1,
            grid=(nb,),
            in_specs=[
                pl.BlockSpec((n, rows), lambda i, o: (0, o[i])),
                pl.BlockSpec((rows, d), lambda i, o: (o[i], 0)),
                pl.BlockSpec((1, rows, d), lambda i, o: (o[i], 0, 0)),
                pl.BlockSpec((n, d), lambda i, o: (0, 0)),
            ],
            out_specs=(
                pl.BlockSpec((1, rows, d), lambda i, o: (i, 0, 0)),
                pl.BlockSpec((d, n), lambda i, o: (0, 0)),
                pl.BlockSpec((8, d), lambda i, o: (0, 0)),
            ),
            scratch_shapes=[pltpu.VMEM((n, d), F32)],
        ),
        out_shape=(sds((nb, rows, d), BF), sds((d, n), BF), sds((8, d), F32)),
        compiler_params=params(),
        cost_estimate=cost(4 * t * d * n, 14 * 2**20),
        name="project_back",
    )(order, gproj, normed, tok_all, wt)


def tokens_back(gn, tok, gain, gmid):
    hat, r = norm_rows(tok.astype(F32))
    e = gn * gain
    m1 = jnp.mean(e, axis=-1, keepdims=True)
    m2 = jnp.mean(e * hat, axis=-1, keepdims=True)
    return (gmid + (e - m1 - hat * m2) * r).astype(BF)


def spans(ids):
    b = ids.reshape(-1, TB)
    low = jnp.min(jnp.where(b < 0, 1000, b), axis=1)
    high = jnp.max(b, axis=1)
    n = b.shape[0]
    k = jnp.arange(n)
    lo = jnp.sum((high[None, :] < low[:, None]) & (k[None, :] <= k[:, None]), axis=1)
    hi = jnp.sum(low[None, :] <= high[:, None], axis=1)
    return jnp.concatenate([lo, hi]).astype(jnp.int32)


def solution(mesh):
    ndp, nmp = mesh.shape["dp"], mesh.shape["mp"]
    ndev, nz = ndp * nmp, ndp // 2

    def permute(v, kind, k=0):
        pairs = []
        for d in range(ndp):
            for m in range(nmp):
                z, y, x, c = d // 2, d % 2, m // 2, m % 2
                if kind == "core":
                    c = 1 - c
                if kind == "x":
                    x = 1 - x
                if kind == "y":
                    y = 1 - y
                if kind == "z":
                    z = (z + k) % nz
                pairs.append((d * nmp + m, (z * 2 + y) * nmp + x * 2 + c))
        return lax.ppermute(v, ("dp", "mp"), pairs)

    def columns(w, first, second):
        if w.shape[0] % 16:
            own = lax.all_gather(w, "dp", axis=0, tiled=True)[None]
            return [own, permute(own, "x")]
        s = jnp.stack([w] + [permute(w, "z", k) for k in range(1, nz)])
        got = {(0, 0): s}
        one = permute(s, first)
        two = permute(s, second)
        both = permute(one, second)
        got[(0, 1)] = one if first == "y" else two
        got[(1, 0)] = two if first == "y" else one
        got[(1, 1)] = both
        return [got[(0, 0)], got[(0, 1)], got[(1, 0)], got[(1, 1)]]

    def body(
        tokens,
        picture_ids,
        w_qkv,
        w_out,
        w_up,
        w_down,
        ln1_gain,
        ln1_bias,
        q_gain,
        k_gain,
        out_bias,
        ln2_gain,
        ln2_bias,
        up_bias,
        down_bias,
        cotangent,
    ):
        rows, d = tokens.shape[1], tokens.shape[2]
        drow = w_qkv.shape[0]
        cols = w_qkv.shape[2]
        heads = cols // HEAD
        unit = w_up.shape[1]
        dp, mp = lax.axis_index("dp"), lax.axis_index("mp")
        z, y, x, c = dp // 2, dp % 2, mp // 2, mp % 2
        tok, cot = tokens[0], cotangent[0]

        vs = [ln1_gain, ln1_bias, q_gain, k_gain, out_bias, ln2_gain, ln2_bias, down_bias, up_bias]
        small = vs[0].shape[0]
        flat = jnp.concatenate(vs)
        used = flat.shape[0]
        vec = jnp.pad(flat, (0, 1024 - used)).reshape(8, 128)
        wcat = jnp.concatenate([w_qkv.reshape(drow, 3 * cols), w_out], axis=1)
        tok_all, w_all, vec_all = gather_all(tok, wcat, vec, ndp, nmp)
        vec_all = vec_all.reshape(nmp, ndp, 1024).transpose(1, 0, 2).reshape(ndev, 1024)
        gain1, shift1, qg, kg, obias, gain2, shift2, dbias = [
            vec_all[:, i * small : (i + 1) * small].reshape(1, d) for i in range(8)
        ]
        ubias = vec_all[:, 8 * small : used].reshape(nmp, unit)
        gains = jnp.concatenate(
            [
                lax.dynamic_slice_in_dim(qg[0], mp * cols, cols),
                lax.dynamic_slice_in_dim(kg[0], mp * cols, cols),
            ]
        ).reshape(2 * cols, 1)

        ups = columns(w_up, "y", "x")
        downs = columns(w_down, "x", "y")
        cot_other = permute(cot, "core")

        normed, raw, low, wt = project(
            tok_all, w_all.reshape(d, 3 * cols + w_out.shape[1]), gain1, shift1, gains, heads
        )
        wo0 = wt[3 * cols :]
        wo1 = permute(wo0, "x")
        wo2, wo3 = permute(wo0, "core"), permute(wo1, "core")
        wos = (wo0, wo1, wo2, wo3)
        ids = picture_ids
        span = spans(ids[0])
        att, lse = attend(span, low, ids, heads)
        att_own = swap(att, True, nmp, 1).reshape(d, rows)
        mid, n2 = middle_part(att_own, wos, tok, obias, gain2, shift2)
        n2_other = permute(n2, "core")
        o_own, o_send, g_own, g_send, dwu, dwd, gbias = feed(
            n2, n2_other, cot, cot_other, ubias, ups, downs, nz
        )
        g_got = permute(g_send, "core")
        gmid, gatt, gwo, sums2 = middle_back(g_own, g_got, mid, cot, att_own, wos, gain2, nmp)
        o_got = permute(o_send, "core")
        result = (mid + o_own + o_got.astype(F32) + dbias).astype(BF)
        dout = swap(gatt, False, nmp, 2)
        gproj, ggain = attend_back(span, low, raw, att, lse, dout, ids, gains, heads)
        order = jnp.stack([mp, x * 2 + 1 - c, (1 - x) * 2 + c, (1 - x) * 2 + 1 - c]).astype(jnp.int32)
        gn, gwq, sums1 = project_back(order, gproj, normed, tok_all, wt[: 3 * cols])
        got = permute(gn[1::2], "core")
        mine = gn[0::2].astype(F32) + got.astype(F32)
        far = permute(mine[1].astype(BF), "x")
        gnormed = mine[0] + far.astype(F32)
        grad_tokens = tokens_back(gnormed, tok, gain1, gmid)

        def pick(v, i):
            return lax.dynamic_index_in_dim(v, i, 0, keepdims=False)

        def along(v, kind):
            i = {"x": None, "y": y}[kind]
            if i is None:
                keep, send = v[0], v[1]
            else:
                keep, send = pick(v, i), pick(v, 1 - i)
            return (keep.astype(F32) + permute(send, kind).astype(F32)).astype(BF)

        def along_z(v):
            total = pick(v, z).astype(F32)
            for k in range(1, nz):
                total = total + permute(pick(v, (z + k) % nz), "z", k).astype(F32)
            return total

        def over_dp(v):
            if drow % 16:
                return lax.psum_scatter(v.astype(F32), "dp", scatter_dimension=0, tiled=True)
            v = v.reshape(nz, 2, drow, v.shape[-1]).transpose(1, 0, 2, 3)
            return along_z(along(v, "y"))

        def reduce_columns(v, y_first):
            if drow % 16 or not y_first:
                return over_dp(along(v, "x"))
            v = v.reshape(2, nz, 2, drow, unit).transpose(2, 0, 1, 3, 4)
            return along_z(along(along(v, "y"), "x"))

        grad_up = reduce_columns(dwu, False)
        grad_down = reduce_columns(dwd, True)
        mine_o = jnp.stack([pick(gwo, mp), pick(gwo, (1 - x) * 2 + c)])
        send_o = jnp.stack([pick(gwo, x * 2 + 1 - c), pick(gwo, (1 - x) * 2 + 1 - c)])
        go = (mine_o.astype(F32) + permute(send_o, "core").astype(F32)).astype(BF)
        go = along(go, "x")
        grad_att = over_dp(jnp.concatenate([gwq, go], axis=1))

        def spread(v, at, size):
            return lax.dynamic_update_slice_in_dim(jnp.zeros((size,), F32), v, at, 0)

        gq = spread(ggain[:cols, 0], mp * cols, d)
        gk = spread(ggain[cols:, 0], mp * cols, d)
        gb = spread(gbias[0, 0], mp * unit, nmp * unit)
        gb = gb + spread(gbias[1, 0], ((1 - x) * 2 + c) * unit, nmp * unit)
        eight = jnp.stack([sums1[0], sums1[1], gq, gk, sums2[0], sums2[1], sums2[2], sums2[3]])
        parts = jnp.concatenate(
            [
                eight.reshape(8, ndev, small).transpose(1, 0, 2).reshape(ndev, 8 * small),
                gb.reshape(ndev, used - 8 * small),
            ],
            axis=1,
        )
        parts = jnp.pad(parts, ((0, 0), (0, 1024 - used))).reshape(ndev, 8, 128)
        tot = vector_sums(parts, ndp, nmp).reshape(1024)
        vgrads = [tot[i * small : (i + 1) * small] for i in range(8)] + [tot[8 * small : used]]

        return (
            result[None],
            grad_tokens[None],
            grad_att[:, : 3 * cols].reshape(drow, 3, cols),
            grad_att[:, 3 * cols :],
            grad_up,
            grad_down,
            vgrads[0],
            vgrads[1],
            vgrads[2],
            vgrads[3],
            vgrads[4],
            vgrads[5],
            vgrads[6],
            vgrads[8],
            vgrads[7],
        )

    vec_spec = P(("dp", "mp"))
    return jax.shard_map(
        body,
        mesh=mesh,
        in_specs=(
            P("dp", "mp", None),
            P("dp", None),
            P("dp", None, "mp"),
            P("dp", "mp"),
            P("dp", "mp"),
            P("dp", "mp"),
        )
        + (vec_spec,) * 9
        + (P("dp", "mp", None),),
        out_specs=(
            P("dp", "mp", None),
            P("dp", "mp", None),
            P("dp", None, "mp"),
            P("dp", "mp"),
            P("dp", "mp"),
            P("dp", "mp"),
        )
        + (vec_spec,) * 9,
        check_vma=False,
    )
```

time: 1020 us -> 388 us (0.38)
  waiting for transfers between devices: 459 us -> 50.3 us
  matrix products: 220 us -> 0 us
  Pallas kernels: 0 us -> 212 us
  blocking collectives: 152 us -> 0 us
  other arithmetic: 99 us -> 25.4 us
  starting transfers between devices: 1.57 us -> 55.5 us
  local copies, waits for them, and re-layouts: 62.7 us -> 40.1 us
  between operations: 16.8 us -> 1.25 us
    reduce_scatter x7 -> x0, waiting for transfers between devices: 287 us -> none  [the longest x1 72.4 us: body(): lax.psum_scatter(grad_qkv_w, 'dp', scatter_dimension=0, tiled=True)]
    dot_general x39 -> x0, matrix products: 216 us -> none  [the longest x8 35.8 us: one_block(): jnp.einsum('qhd,khd->hqk', query_block, key_rows, preferred_element_type=...]
    pallas_call x0 -> x11, Pallas kernels: none -> 212 us  [the longest x1 38.6 us: gather_all(): pl.pallas_call(functools.partial(gather_kernel, nz, nc), out_shape=(sds((...]
    all_gather x6 -> x0, waiting for transfers between devices: 110 us -> none  [the longest x1 28.5 us: body(): grad_rows = lax.all_gather(cotangent, 'mp', axis=1, tiled=True)]
    unnamed x2 -> x0, blocking collectives: 83.4 us -> none
    all_gather x2 -> x0, blocking collectives: 68.4 us -> none  [the longest x1 37.2 us: body(): lax.all_gather(w_qkv, 'dp', axis=0, tiled=True)]
    unnamed x15 -> x0, waiting for transfers between devices: 62.6 us -> none
    ppermute x0 -> x37, starting transfers between devices: none -> 55.5 us  [permute(): return lax.ppermute(v, ('dp', 'mp'), pairs)]
  transfers between devices with their start and end apart: 14 -> 37, of which waited for: 11 -> 9; matrix products, arithmetic and copies ran while one was open for 7% -> 15% of each run, Pallas kernels for 0% -> 48%
where the time goes in v1:
time: 388 us; the launch traced here: 384 us
  Pallas kernels  212 us (55%)
  starting transfers between devices  55.5 us (14%)
  waiting for transfers between devices  50.3 us (13%)
  local copies, waits for them, and re-layouts  40.1 us (10%)
  other arithmetic  25.4 us (7%)
    ppermute x37, starting transfers between devices, permute(): return lax.ppermute(v, ('dp', 'mp'), pairs)  55.5 us
    ppermute x37, waiting for transfers between devices, permute(): return lax.ppermute(v, ('dp', 'mp'), pairs)  50.3 us
    pallas_call x1, Pallas kernels, gather_all(): pl.pallas_call(functools.partial(gather_kernel, nz, nc), out_shape=(sds((...  38.6 us
    pallas_call x1, Pallas kernels, attend_back(): pl.pallas_call(functools.partial(attend_back_kernel, heads, t // TB), out...  34.5 us
    pallas_call x1, Pallas kernels, feed(): pl.pallas_call(functools.partial(feed_kernel, len(pieces), nz), out_shape...  28.1 us
    pallas_call x2, Pallas kernels, swap(): pl.pallas_call(functools.partial(swap_kernel, forward, nmp), out_shape=sd...  27.3 us
    pallas_call x1, Pallas kernels, vector_sums(): pl.pallas_call(functools.partial(vector_kernel, ndp, nmp), out_shape=sds(...  27.3 us
    pallas_call x1, Pallas kernels, attend(): pl.pallas_call(functools.partial(attend_kernel, heads, t // TB), out_shap...  25.2 us
  transfers between devices with their start and end apart: 37, of which 9 were waited for; matrix products, arithmetic and copies ran while one was open for 15% of the time, Pallas kernels for 48%

profile of v1, /device:TPU:0, one launch (start us, length us, event | category | flops | bytes accessed | tf_op | source)
XLA Modules:
  0.0 384.0 jit_solution(5175486701416744357)
XLA Ops:
  0.6 3.1 collective-permute-start.5
  3.7 2.1 collective-permute-start.7
  5.8 3.8 collective-permute-start.13
  11.6 1.4 reduce.11
  14.2 1.5 pad_maximum_fusion.4.w
  15.8 38.6 %gather_start.1 = (bf16[4,512,768]{2,1,0:T(8,128)(2,1)}, bf16[8,96,768]{2,1,0:T(8,128)(2,1)}, f32[4,8,8,128]{3,2,1,0:T(8,128)}) custom-call(bf16[512,768]{1,0:T(8,128)(2,1)} %bitcast.120, bf16[96,768]{1,0:T(8,128)(2,1)} %pad_maximum_fusion.4.w, f32[8,128]{1,0:T(8,128)} %pad_bitcast_fusion.vec), custom_call_target="tpu_custom_call" | custom-call | tf_op jit(solution)/shard_map/gather_start/pallas_call | solution.py:150
  58.1 9.1 %project_qkv.1 = (bf16[2048,768]{1,0:T(8,128)(2,1)}, f32[384,2048]{1,0:T(8,128)}, bf16[576,2048]{1,0:T(8,128)(2,1)}, bf16[768,768]{1,0:T(8,128)(2,1)}) custom-call(bf16[4,512,768]{2,1,0:T(8,128)(2,1)} %get-tuple-element.42.tok, bf16[768,768]{1,0:T(8,128)(2,1)} %bitcast.149, f32[1,768]{1,0:T(1,128)} %reshape.165.gain, f32[1,768]{1,0:T(1,128)} %reshape.166.shift, ...), custom_call_target="tpu_custom_call" | custom-call | flops 1811939328 | bytes 12582912 | tf_op jit(solution)/shard_map/project_qkv/pallas_call | solution.py:291
  68.6 1.6 collective-permute-start.6
  72.2 1.5 collective-permute-start.15
  74.2 4.7 %collective-permute-done.6 = bf16[96,768]{1,0:T(8,128)(2,1)S(1)} collective-permute-done((bf16[96,768]{1,0:T(8,128)(2,1)S(1)}, bf16[96,768]{1,0:T(8,128)(2,1)S(1)}, u32[]{:S(2)}, u32[]{:S(2)}) %collective-permute-start.6) | collective-permute-done | bytes 147488 | tf_op jit(solution)/shard_map/ppermute | solution.py:763
  79.8 1.5 collective-permute-start.8
  81.3 25.2 %attend.1 = (bf16[192,2048]{1,0:T(8,128)(2,1)}, f32[8,2048]{1,0:T(8,128)}) custom-call(s32[16]{0:T(128)} %pad_add_fusion.span, bf16[576,2048]{1,0:T(8,128)(2,1)} %get-tuple-element.45.low, s32[1,2048]{1,0:T(1,128)} %ids.3), custom_call_target="tpu_custom_call" | custom-call | flops 12000000000 | bytes 4194304 | tf_op jit(solution)/shard_map/attend/pallas_call | solution.py:386
  108.6 9.9 %swap_fwd.1 = bf16[4,192,512]{2,1,0:T(8,128)(2,1)} custom-call(bf16[192,2048]{1,0:T(8,128)(2,1)} %get-tuple-element.46.src.att), custom_call_target="tpu_custom_call" | custom-call | tf_op jit(solution)/shard_map/swap_fwd/pallas_call | solution.py:210
  118.5 1.8 collective-permute-start.4
  121.1 4.1 %middle.1 = (f32[512,768]{1,0:T(8,128)}, bf16[512,768]{1,0:T(8,128)(2,1)}) custom-call(bf16[768,512]{1,0:T(8,128)(2,1)} %bitcast.122, bf16[192,768]{1,0:T(8,128)(2,1)} %copy-done.5, bf16[192,768]{1,0:T(8,128)(2,1)} %copy-done.14, bf16[192,768]{1,0:T(8,128)(2,1)} %copy-done.15, bf16[192,768]{1,0:T(8,128)(2,1)} %copy-done.16, bf16[512,768]{1,0:T(8,128)(2,1)} %bitcast.121, ...), custom_call_target="tpu_custom_call" | custom-call | flops 603979776 | bytes 6291456 | tf_op jit(solution)/shard_map/middle/pallas_call | solution.py:516
  126.7 8.3 %collective-permute-start.16 = (bf16[4,96,768]{2,1,0:T(8,128)(2,1)}, bf16[4,96,768]{2,1,0:T(8,128)(2,1)}, u32[]{:S(2)}, u32[]{:S(2)}) collective-permute-start(bf16[4,96,768]{2,1,0:T(8,128)(2,1)} %collective-permute-done.15.refs_11_), channel_id=1, source_target_pairs={{0,4},{1,5},{2,6},{3,7},{4,0},{5,1},{6,2},{7,3},{8,12},{9,13},{10,... | collective-permute-start | bytes 1769480 | tf_op jit(solution)/shard_map/ppermute | solution.py:763
  135.0 1.6 collective-permute-start.10
  137.7 4.9 %collective-permute-done.9.refs_7_ = bf16[4,96,768]{2,1,0:T(8,128)(2,1)S(1)} collective-permute-done((bf16[4,96,768]{2,1,0:T(8,128)(2,1)}, bf16[4,96,768]{2,1,0:T(8,128)(2,1)S(1)}, u32[]{:S(2)}, u32[]{:S(2)}) %collective-permute-start.9) | collective-permute-done | bytes 589856 | tf_op jit(solution)/shard_map/ppermute | solution.py:763
  142.5 6.5 %collective-permute-done.16.refs_12_ = bf16[4,96,768]{2,1,0:T(8,128)(2,1)} collective-permute-done((bf16[4,96,768]{2,1,0:T(8,128)(2,1)}, bf16[4,96,768]{2,1,0:T(8,128)(2,1)}, u32[]{:S(2)}, u32[]{:S(2)}) %collective-permute-start.16) | collective-permute-done | bytes 589856 | tf_op jit(solution)/shard_map/ppermute | solution.py:763
  149.0 5.8 %collective-permute-done.10.refs_8_ = bf16[4,96,768]{2,1,0:T(8,128)(2,1)} collective-permute-done((bf16[4,96,768]{2,1,0:T(8,128)(2,1)}, bf16[4,96,768]{2,1,0:T(8,128)(2,1)}, u32[]{:S(2)}, u32[]{:S(2)}) %collective-permute-start.10) | collective-permute-done | bytes 589856 | tf_op jit(solution)/shard_map/ppermute | solution.py:763
  154.9 28.1 %feed_forward.1 = (f32[512,768]{1,0:T(8,128)}, bf16[512,768]{1,0:T(8,128)(2,1)}, f32[512,768]{1,0:T(8,128)}, bf16[512,768]{1,0:T(8,128)(2,1)}, bf16[2,768,768]{2...) custom-call(bf16[512,768]{1,0:T(8,128)(2,1)} %get-tuple-element.49.refs_0_, ...), custom_call_target="tpu_custom_call" | custom-call | flops 14495514624 | bytes 23068672 | tf_op jit(solution)/shard_map/feed_forward/pallas_call | solution.py:647
  188.0 2.4 slice_bitcast_fusion.1
  192.1 8.3 %collective-permute-start.32 = (bf16[2,4,96,768]{3,2,1,0:T(8,128)(2,1)}, bf16[2,4,96,768]{3,2,1,0:T(8,128)(2,1)}, u32[]{:S(2)}, u32[]{:S(2)}) collective-permute-start(bf16[2,4,96,768]{3,2,1,0:T(8,128)(2,1)} %dynamic-slice_bitcast_fusion), channel_id=1, source_target_pairs={{0,4},{1,5},{2,6},{3,7},{4,0},{5,1},{6,2},{7,3},{8,12},{9,13},{10,... | collective-permute-start | bytes 3538952 | tf_op jit(solution)/shard_map/ppermute | solution.py:763
  200.4 6.7 %middle_back.1 = (f32[512,768]{1,0:T(8,128)}, bf16[4,192,512]{2,1,0:T(8,128)(2,1)}, bf16[4,768,192]{2,1,0:T(8,128)(2,1)}, f32[8,768]{1,0:T(8,128)}) custom-call(f32[512,768]{1,0:T(8,128)} %get-tuple-element.52.g0, bf16[512,768]{1,0:T(8,128)(2,1)} %collective-permute-done.18.g1, f32[512,768]{1,0:T(8,128)} %get-tuple-element.48.mid, ...), custom_call_target="tpu_custom_call" | custom-call | flops 1207959552 | bytes 10485760 | tf_op jit(solution)/shard_map/middle_back/pallas_call | solution.py:556
  207.8 17.4 %swap_bwd.1.dout = bf16[192,2048]{1,0:T(8,128)(2,1)} custom-call(bf16[4,192,512]{2,1,0:T(8,128)(2,1)} %get-tuple-element.57.src), custom_call_target="tpu_custom_call" | custom-call | tf_op jit(solution)/shard_map/swap_bwd/pallas_call | solution.py:210
  225.2 34.5 %attend_back.1 = (bf16[576,2048]{1,0:T(8,128)(2,1)}, f32[384,1]{1,0:T(8,128)}) custom-call(s32[16]{0:T(128)} %pad_add_fusion.span, bf16[576,2048]{1,0:T(8,128)(2,1)} %get-tuple-element.45.low, f32[384,2048]{1,0:T(8,128)} %get-tuple-element.55.raw, bf16[192,2048]{1,0:T(8,128)(2,1)} %get-tuple-element.46.src.att, f32[8,2048]{1,0:T(8,128)} %get-tuple-element.56.lse, ...), custom_call_target="tpu_custom_call" | custom-call | flops 30000001024 | bytes 12582912 | tf_op jit(solution)/shard_map/attend_back/pallas_call | solution.py:477
  259.8 10.8 %project_back.1 = (bf16[4,512,768]{2,1,0:T(8,128)(2,1)}, bf16[768,576]{1,0:T(8,128)(2,1)}, f32[8,768]{1,0:T(8,128)}) custom-call(s32[4]{0:T(128)} %pad_add_fusion.1.order, bf16[576,2048]{1,0:T(8,128)(2,1)} %get-tuple-element.58.gproj, bf16[2048,768]{1,0:T(8,128)(2,1)} %get-tuple-element.59.normed, bf16[4,512,768]{2,1,0:T(8,128)(2,1)} %get-tuple-element.42.tok, ...), custom_call_target="tpu_custom_call" | custom-call | flops 3623878656 | bytes 14680064 | tf_op jit(solution)/shard_map/project_back/pallas_call | solution.py:701
  274.6 2.4 fusion.17
  277.8 27.3 %vector_sums.1 = f32[8,128]{1,0:T(8,128)} custom-call(f32[32,8,128]{2,1,0:T(8,128)} %bitcast.136), custom_call_target="tpu_custom_call" | custom-call | tf_op jit(solution)/shard_map/vector_sums/pallas_call | solution.py:243
  306.7 2.8 slice.133
  310.6 1.6 fusion.1
  313.1 1.7 collective-permute-start.28
  317.8 1.6 fusion
  321.0 7.5 %collective-permute-done.22 = bf16[768,192]{1,0:T(8,128)(2,1)S(1)} collective-permute-done((bf16[768,192]{1,0:T(8,128)(2,1)S(1)}, bf16[768,192]{1,0:T(8,128)(2,1)S(1)}, u32[]{:S(2)}, u32[]{:S(2)}) %collective-permute-start.22) | collective-permute-done | bytes 294944 | tf_op jit(solution)/shard_map/ppermute | solution.py:763
  330.0 2.3 copy.77
  334.9 2.7 collective-permute-start.31
  337.6 2.4 collective-permute-done.33
  340.0 1.6 collective-permute-start.30
  344.2 2.6 collective-permute-start.36
  346.7 7.1 %collective-permute-done.30 = bf16[96,768]{1,0:T(8,128)(2,1)S(1)} collective-permute-done((bf16[96,768]{1,0:T(8,128)(2,1)S(1)}, bf16[96,768]{1,0:T(8,128)(2,1)S(1)}, u32[]{:S(2)}, u32[]{:S(2)}) %collective-permute-start.30) | collective-permute-done | bytes 147488 | tf_op jit(solution)/shard_map/ppermute | solution.py:763
  354.6 1.4 copy.71
  356.1 2.2 convert_add_fusion
  360.4 3.8 collective-permute-start.26
  365.3 1.7 fusion.24
  367.0 3.0 collective-permute-done.24
  370.1 8.3 %collective-permute-done.25 = bf16[96,768]{0,1:T(8,128)(2,1)S(1)} collective-permute-done((bf16[96,768]{0,1:T(8,128)(2,1)S(1)}, bf16[96,768]{0,1:T(8,128)(2,1)S(1)}, u32[]{:S(2)}, u32[]{:S(2)}) %collective-permute-start.25) | collective-permute-done | bytes 147488 | tf_op jit(solution)/shard_map/ppermute | solution.py:763
  380.2 2.2 fusion.27
  382.5 1.5 fusion.19
  (193 shorter events, 49.9 us)
Async XLA Ops:
  0.6 71.5 %collective-permute-start.5 = (bf16[96,768]{1,0:T(8,128)(2,1)}, bf16[96,768]{1,0:T(8,128)(2,1)S(1)}, u32[]{:S(2)}, u32[]{:S(2)}) collective-permute-start(bf16[96,768]{1,0:T(8,128)(2,1)} %param.20), channel_id=1, source_target_pairs={{0,8},{1,9},{2,10},{3,11},{4,12},{5,13},{6,14},{7,15},{8,16},{9,17... | collective-permute-start | bytes 442376 | tf_op jit(solution)/shard_map/ppermute | solution.py:763
  3.7 70.0 %collective-permute-start.7 = (bf16[96,768]{1,0:T(8,128)(2,1)}, bf16[96,768]{1,0:T(8,128)(2,1)S(1)}, u32[]{:S(2)}, u32[]{:S(2)}) collective-permute-start(bf16[96,768]{1,0:T(8,128)(2,1)} %param.20), channel_id=1, source_target_pairs={{0,24},{1,25},{2,26},{3,27},{4,28},{5,29},{6,30},{7,31},{8,0},{9,1... | collective-permute-start | bytes 442376 | tf_op jit(solution)/shard_map/ppermute | solution.py:763
  5.8 62.7 %collective-permute-start.11 = (bf16[96,768]{1,0:T(8,128)(2,1)}, bf16[96,768]{1,0:T(8,128)(2,1)S(1)}, u32[]{:S(2)}, u32[]{:S(2)}) collective-permute-start(bf16[96,768]{1,0:T(8,128)(2,1)} %param.21), channel_id=1, source_target_pairs={{0,8},{1,9},{2,10},{3,11},{4,12},{5,13},{6,14},{7,15},{8,16},{9,17... | collective-permute-start | bytes 442376 | tf_op jit(solution)/shard_map/ppermute | solution.py:763
  5.8 64.3 %collective-permute-start.13 = (bf16[96,768]{1,0:T(8,128)(2,1)}, bf16[96,768]{1,0:T(8,128)(2,1)S(1)}, u32[]{:S(2)}, u32[]{:S(2)}) collective-permute-start(bf16[96,768]{1,0:T(8,128)(2,1)} %param.21), channel_id=1, source_target_pairs={{0,24},{1,25},{2,26},{3,27},{4,28},{5,29},{6,30},{7,31},{8,0},{9,1... | collective-permute-start | bytes 442376 | tf_op jit(solution)/shard_map/ppermute | solution.py:763
  9.6 61.6 %collective-permute-start.12 = (bf16[96,768]{1,0:T(8,128)(2,1)}, bf16[96,768]{1,0:T(8,128)(2,1)S(1)}, u32[]{:S(2)}, u32[]{:S(2)}) collective-permute-start(bf16[96,768]{1,0:T(8,128)(2,1)} %param.21), channel_id=1, source_target_pairs={{0,16},{1,17},{2,18},{3,19},{4,20},{5,21},{6,22},{7,23},{8,24},{9,... | collective-permute-start | bytes 442376 | tf_op jit(solution)/shard_map/ppermute | solution.py:763
  58.1 13.2 %copy-start.20 = (bf16[96,768]{1,0:T(8,128)(2,1)S(1)}, bf16[96,768]{1,0:T(8,128)(2,1)}, u32[]{:S(2)}) copy-start(bf16[96,768]{1,0:T(8,128)(2,1)} %param.21) | copy-start | bytes 442372
  68.5 38.0 %copy-start.5 = (bf16[192,768]{1,0:T(8,128)(2,1)}, bf16[192,768]{1,0:T(8,128)(2,1)S(1)}, u32[]{:S(2)}) copy-start(bf16[192,768]{1,0:T(8,128)(2,1)S(1)} %slice.125.w0) | copy-start | bytes 884740
  68.6 10.3 %collective-permute-start.6 = (bf16[96,768]{1,0:T(8,128)(2,1)S(1)}, bf16[96,768]{1,0:T(8,128)(2,1)S(1)}, u32[]{:S(2)}, u32[]{:S(2)}) collective-permute-start(bf16[96,768]{1,0:T(8,128)(2,1)S(1)} %copy-done.21), channel_id=1, source_target_pairs={{0,16},{1,17},{2,18},{3,19},{4,20},{5,21},{6,22},{7,23},{8,24},{9,... | collective-permute-start | bytes 442376 | tf_op jit(solution)/shard_map/ppermute | solution.py:763
  70.1 11.2 %collective-permute-start = (bf16[192,768]{1,0:T(8,128)(2,1)S(1)}, bf16[192,768]{1,0:T(8,128)(2,1)S(1)}, u32[]{:S(2)}, u32[]{:S(2)}) collective-permute-start(bf16[192,768]{1,0:T(8,128)(2,1)S(1)} %slice.125.w0), channel_id=1, source_target_pairs={{0,2},{1,3},{2,0},{3,1},{4,6},{5,7},{6,4},{7,5},{8,10},{9,11},{10,... | collective-permute-start | bytes 884744 | tf_op jit(solution)/shard_map/ppermute | solution.py:763
  71.3 47.2 %collective-permute-start.1 = (bf16[192,768]{1,0:T(8,128)(2,1)S(1)}, bf16[192,768]{1,0:T(8,128)(2,1)S(1)}, u32[]{:S(2)}, u32[]{:S(2)}) collective-permute-start(bf16[192,768]{1,0:T(8,128)(2,1)S(1)} %slice.125.w0), channel_id=1, source_target_pairs={{0,1},{1,0},{2,3},{3,2},{4,5},{5,4},{6,7},{7,6},{8,9},{9,8},{10,11... | collective-permute-start | bytes 884744 | tf_op jit(solution)/shard_map/ppermute | solution.py:763
  72.2 53.9 %collective-permute-start.15 = (bf16[4,96,768]{2,1,0:T(8,128)(2,1)}, bf16[4,96,768]{2,1,0:T(8,128)(2,1)}, u32[]{:S(2)}, u32[]{:S(2)}) collective-permute-start(bf16[4,96,768]{2,1,0:T(8,128)(2,1)} %pad_maximum_fusion.3.refs_9_), channel_id=1, source_target_pairs={{0,2},{1,3},{2,0},{3,1},{4,6},{5,7},{6,4},{7,5},{8,10},{9,11},{10,... | collective-permute-start | bytes 1769480 | tf_op jit(solution)/shard_map/ppermute | solution.py:763
  73.7 53.0 %collective-permute-start.14 = (bf16[4,96,768]{2,1,0:T(8,128)(2,1)}, bf16[4,96,768]{2,1,0:T(8,128)(2,1)}, u32[]{:S(2)}, u32[]{:S(2)}) collective-permute-start(bf16[4,96,768]{2,1,0:T(8,128)(2,1)} %pad_maximum_fusion.3.refs_9_), channel_id=1, source_target_pairs={{0,4},{1,5},{2,6},{3,7},{4,0},{5,1},{6,2},{7,3},{8,12},{9,13},{10,... | collective-permute-start | bytes 1769480 | tf_op jit(solution)/shard_map/ppermute | solution.py:763
  79.8 55.2 %collective-permute-start.8 = (bf16[4,96,768]{2,1,0:T(8,128)(2,1)}, bf16[4,96,768]{2,1,0:T(8,128)(2,1)}, u32[]{:S(2)}, u32[]{:S(2)}) collective-permute-start(bf16[4,96,768]{2,1,0:T(8,128)(2,1)} %pad_maximum_fusion.2.refs_5_), channel_id=1, source_target_pairs={{0,4},{1,5},{2,6},{3,7},{4,0},{5,1},{6,2},{7,3},{8,12},{9,13},{10,... | collective-permute-start | bytes 1769480 | tf_op jit(solution)/shard_map/ppermute | solution.py:763
  81.3 25.2 %copy-start.14 = (bf16[192,768]{1,0:T(8,128)(2,1)}, bf16[192,768]{1,0:T(8,128)(2,1)S(1)}, u32[]{:S(2)}) copy-start(bf16[192,768]{1,0:T(8,128)(2,1)S(1)} %collective-permute-done.w1) | copy-start | bytes 884740
  81.3 39.0 %collective-permute-start.2 = (bf16[192,768]{1,0:T(8,128)(2,1)S(1)}, bf16[192,768]{1,0:T(8,128)(2,1)S(1)}, u32[]{:S(2)}, u32[]{:S(2)}) collective-permute-start(bf16[192,768]{1,0:T(8,128)(2,1)S(1)} %collective-permute-done.w1), channel_id=1, source_target_pairs={{0,1},{1,0},{2,3},{3,2},{4,5},{5,4},{6,7},{7,6},{8,9},{9,8},{10,11... | collective-permute-start | bytes 884744 | tf_op jit(solution)/shard_map/ppermute | solution.py:763
  106.5 12.0 %copy-start.18 = (bf16[1,512,768]{2,1,0:T(8,128)(2,1)S(1)}, bf16[1,512,768]{2,1,0:T(8,128)(2,1)}, u32[]{:S(2)}) copy-start(bf16[1,512,768]{2,1,0:T(8,128)(2,1)} %param.31) | copy-start | bytes 2359300
  118.5 24.0 %collective-permute-start.4 = (bf16[512,768]{1,0:T(8,128)(2,1)S(1)}, bf16[512,768]{1,0:T(8,128)(2,1)}, u32[]{:S(2)}, u32[]{:S(2)}) collective-permute-start(bf16[512,768]{1,0:T(8,128)(2,1)S(1)} %bitcast.132), channel_id=1, source_target_pairs={{0,1},{1,0},{2,3},{3,2},{4,5},{5,4},{6,7},{7,6},{8,9},{9,8},{10,11... | collective-permute-start | bytes 2359304 | tf_op jit(solution)/shard_map/ppermute | solution.py:763
  125.2 29.7 %collective-permute-start.3 = (bf16[512,768]{1,0:T(8,128)(2,1)}, bf16[512,768]{1,0:T(8,128)(2,1)}, u32[]{:S(2)}, u32[]{:S(2)}) collective-permute-start(bf16[512,768]{1,0:T(8,128)(2,1)} %get-tuple-element.49.refs_0_), channel_id=1, source_target_pairs={{0,1},{1,0},{2,3},{3,2},{4,5},{5,4},{6,7},{7,6},{8,9},{9,8},{10,11... | collective-permute-start | bytes 2359304 | tf_op jit(solution)/shard_map/ppermute | solution.py:763
  126.1 16.4 %collective-permute-start.9 = (bf16[4,96,768]{2,1,0:T(8,128)(2,1)}, bf16[4,96,768]{2,1,0:T(8,128)(2,1)S(1)}, u32[]{:S(2)}, u32[]{:S(2)}) collective-permute-start(bf16[4,96,768]{2,1,0:T(8,128)(2,1)} %pad_maximum_fusion.2.refs_5_), channel_id=1, source_target_pairs={{0,2},{1,3},{2,0},{3,1},{4,6},{5,7},{6,4},{7,5},{8,10},{9,11},{10,... | collective-permute-start | bytes 1769480 | tf_op jit(solution)/shard_map/ppermute | solution.py:763
  126.7 22.3 %collective-permute-start.16 = (bf16[4,96,768]{2,1,0:T(8,128)(2,1)}, bf16[4,96,768]{2,1,0:T(8,128)(2,1)}, u32[]{:S(2)}, u32[]{:S(2)}) collective-permute-start(bf16[4,96,768]{2,1,0:T(8,128)(2,1)} %collective-permute-done.15.refs_11_), channel_id=1, source_target_pairs={{0,4},{1,5},{2,6},{3,7},{4,0},{5,1},{6,2},{7,3},{8,12},{9,13},{10,... | collective-permute-start | bytes 1769480 | tf_op jit(solution)/shard_map/ppermute | solution.py:763
  135.0 19.8 %collective-permute-start.10 = (bf16[4,96,768]{2,1,0:T(8,128)(2,1)}, bf16[4,96,768]{2,1,0:T(8,128)(2,1)}, u32[]{:S(2)}, u32[]{:S(2)}) collective-permute-start(bf16[4,96,768]{2,1,0:T(8,128)(2,1)} %collective-permute-done.8.refs_6_), channel_id=1, source_target_pairs={{0,2},{1,3},{2,0},{3,1},{4,6},{5,7},{6,4},{7,5},{8,10},{9,11},{10,... | collective-permute-start | bytes 1769480 | tf_op jit(solution)/shard_map/ppermute | solution.py:763
  136.7 46.3 %copy-start.24 = (f32[512]{0:T(512)}, f32[512]{0:T(512)S(1)}, u32[]{:S(2)}) copy-start(f32[512]{0:T(512)S(1)} %broadcast_multiply_fusion.1) | copy-start | bytes 6148
  137.6 46.7 %copy-start.13 = (bf16[768,768]{1,0:T(8,128)(2,1)S(1)}, bf16[768,768]{1,0:T(8,128)(2,1)}, u32[]{:S(2)}) copy-start(bf16[768,768]{1,0:T(8,128)(2,1)} %get-tuple-element.47) | copy-start | bytes 3538948
  142.5 12.3 %copy-start.29 = (bf16[4,96,768]{2,1,0:T(8,128)(2,1)}, bf16[4,96,768]{2,1,0:T(8,128)(2,1)S(1)}, u32[]{:S(2)}) copy-start(bf16[4,96,768]{2,1,0:T(8,128)(2,1)S(1)} %collective-permute-done.9.refs_7_) | copy-start | bytes 1769476
  183.0 17.4 %collective-permute-start.18 = (bf16[512,768]{1,0:T(8,128)(2,1)}, bf16[512,768]{1,0:T(8,128)(2,1)}, u32[]{:S(2)}, u32[]{:S(2)}) collective-permute-start(bf16[512,768]{1,0:T(8,128)(2,1)} %get-tuple-element.53), channel_id=1, source_target_pairs={{0,1},{1,0},{2,3},{3,2},{4,5},{5,4},{6,7},{7,6},{8,9},{9,8},{10,11... | collective-permute-start | bytes 2359304 | tf_op jit(solution)/shard_map/ppermute | solution.py:763
  187.6 85.5 %collective-permute-start.17 = (bf16[512,768]{1,0:T(8,128)(2,1)}, bf16[512,768]{1,0:T(8,128)(2,1)}, u32[]{:S(2)}, u32[]{:S(2)}) collective-permute-start(bf16[512,768]{1,0:T(8,128)(2,1)} %get-tuple-element.51), channel_id=1, source_target_pairs={{0,1},{1,0},{2,3},{3,2},{4,5},{5,4},{6,7},{7,6},{8,9},{9,8},{10,11... | collective-permute-start | bytes 2359304 | tf_op jit(solution)/shard_map/ppermute | solution.py:763
  190.5 120.1 %collective-permute-start.27 = (bf16[768,768]{1,0:T(8,128)(2,1)}, bf16[768,768]{1,0:T(8,128)(2,1)}, u32[]{:S(2)}, u32[]{:S(2)}) collective-permute-start(bf16[768,768]{1,0:T(8,128)(2,1)} %slice_bitcast_fusion.1), channel_id=1, source_target_pairs={{0,2},{1,3},{2,0},{3,1},{4,6},{5,7},{6,4},{7,5},{8,10},{9,11},{10,... | collective-permute-start | bytes 3538952 | tf_op jit(solution)/shard_map/ppermute | solution.py:763
  192.1 125.1 %collective-permute-start.32 = (bf16[2,4,96,768]{3,2,1,0:T(8,128)(2,1)}, bf16[2,4,96,768]{3,2,1,0:T(8,128)(2,1)}, u32[]{:S(2)}, u32[]{:S(2)}) collective-permute-start(bf16[2,4,96,768]{3,2,1,0:T(8,128)(2,1)} %dynamic-slice_bitcast_fusion), channel_id=1, source_target_pairs={{0,4},{1,5},{2,6},{3,7},{4,0},{5,1},{6,2},{7,3},{8,12},{9,13},{10,... | collective-permute-start | bytes 3538952 | tf_op jit(solution)/shard_map/ppermute | solution.py:763
  259.8 13.0 %copy-start.12 = (bf16[4,768,192]{2,1,0:T(8,128)(2,1)S(1)}, bf16[4,768,192]{2,1,0:T(8,128)(2,1)}, u32[]{:S(2)}) copy-start(bf16[4,768,192]{2,1,0:T(8,128)(2,1)} %get-tuple-element.62) | copy-start | bytes 3538948
  306.6 8.3 %collective-permute-start.21 = (bf16[2,768,192]{1,2,0:T(8,128)(2,1)S(1)}, bf16[2,768,192]{1,2,0:T(8,128)(2,1)}, u32[]{:S(2)}, u32[]{:S(2)}) collective-permute-start(bf16[2,768,192]{1,2,0:T(8,128)(2,1)S(1)} %copy.68), channel_id=1, source_target_pairs={{0,1},{1,0},{2,3},{3,2},{4,5},{5,4},{6,7},{7,6},{8,9},{9,8},{10,11... | collective-permute-start | bytes 1769480 | tf_op jit(solution)/shard_map/ppermute | solution.py:763
  309.5 46.5 %collective-permute-start.19 = (bf16[2,512,768]{2,1,0:T(8,128)(2,1)}, bf16[2,512,768]{2,1,0:T(8,128)(2,1)}, u32[]{:S(2)}, u32[]{:S(2)}) collective-permute-start(bf16[2,512,768]{2,1,0:T(8,128)(2,1)} %slice.133), channel_id=1, source_target_pairs={{0,1},{1,0},{2,3},{3,2},{4,5},{5,4},{6,7},{7,6},{8,9},{9,8},{10,11... | collective-permute-start | bytes 4718600 | tf_op jit(solution)/shard_map/ppermute | solution.py:763
  313.1 19.4 %collective-permute-start.28 = (bf16[4,96,768]{2,1,0:T(8,128)(2,1)}, bf16[4,96,768]{2,1,0:T(8,128)(2,1)}, u32[]{:S(2)}, u32[]{:S(2)}) collective-permute-start(bf16[4,96,768]{2,1,0:T(8,128)(2,1)} %dynamic-slice_bitcast_fusion.1), channel_id=1, source_target_pairs={{0,4},{1,5},{2,6},{3,7},{4,0},{5,1},{6,2},{7,3},{8,12},{9,13},{10,... | collective-permute-start | bytes 1769480 | tf_op jit(solution)/shard_map/ppermute | solution.py:763
  316.4 12.1 %collective-permute-start.22 = (bf16[768,192]{1,0:T(8,128)(2,1)S(1)}, bf16[768,192]{1,0:T(8,128)(2,1)S(1)}, u32[]{:S(2)}, u32[]{:S(2)}) collective-permute-start(bf16[768,192]{1,0:T(8,128)(2,1)S(1)} %slice_bitcast_fusion.4), channel_id=1, source_target_pairs={{0,2},{1,3},{2,0},{3,1},{4,6},{5,7},{6,4},{7,5},{8,10},{9,11},{10,... | collective-permute-start | bytes 884744 | tf_op jit(solution)/shard_map/ppermute | solution.py:763
  320.3 19.7 %collective-permute-start.33 = (bf16[4,96,768]{2,1,0:T(8,128)(2,1)}, bf16[4,96,768]{2,1,0:T(8,128)(2,1)}, u32[]{:S(2)}, u32[]{:S(2)}) collective-permute-start(bf16[4,96,768]{2,1,0:T(8,128)(2,1)} %slice_bitcast_fusion.2), channel_id=1, source_target_pairs={{0,2},{1,3},{2,0},{3,1},{4,6},{5,7},{6,4},{7,5},{8,10},{9,11},{10,... | collective-permute-start | bytes 1769480 | tf_op jit(solution)/shard_map/ppermute | solution.py:763
  332.2 22.4 %collective-permute-start.23 = (bf16[4,96,768]{2,1,0:T(8,128)(2,1)}, bf16[4,96,768]{2,1,0:T(8,128)(2,1)}, u32[]{:S(2)}, u32[]{:S(2)}) collective-permute-start(bf16[4,96,768]{2,1,0:T(8,128)(2,1)} %get-tuple-element.129), channel_id=1, source_target_pairs={{0,4},{1,5},{2,6},{3,7},{4,0},{5,1},{6,2},{7,3},{8,12},{9,13},{10,... | collective-permute-start | bytes 1769480 | tf_op jit(solution)/shard_map/ppermute | solution.py:763
  333.8 9.1 %collective-permute-start.29 = (bf16[96,768]{1,0:T(8,128)(2,1)S(1)}, bf16[96,768]{1,0:T(8,128)(2,1)S(1)}, u32[]{:S(2)}, u32[]{:S(2)}) collective-permute-start(bf16[96,768]{1,0:T(8,128)(2,1)S(1)} %get-tuple-element.136), channel_id=1, source_target_pairs={{0,8},{1,9},{2,10},{3,11},{4,12},{5,13},{6,14},{7,15},{8,16},{9,17... | collective-permute-start | bytes 442376 | tf_op jit(solution)/shard_map/ppermute | solution.py:763
  334.9 9.2 %collective-permute-start.31 = (bf16[96,768]{1,0:T(8,128)(2,1)S(1)}, bf16[96,768]{1,0:T(8,128)(2,1)S(1)}, u32[]{:S(2)}, u32[]{:S(2)}) collective-permute-start(bf16[96,768]{1,0:T(8,128)(2,1)S(1)} %get-tuple-element.137), channel_id=1, source_target_pairs={{0,24},{1,25},{2,26},{3,27},{4,28},{5,29},{6,30},{7,31},{8,0},{9,1... | collective-permute-start | bytes 442376 | tf_op jit(solution)/shard_map/ppermute | solution.py:763
  340.0 13.8 %collective-permute-start.30 = (bf16[96,768]{1,0:T(8,128)(2,1)S(1)}, bf16[96,768]{1,0:T(8,128)(2,1)S(1)}, u32[]{:S(2)}, u32[]{:S(2)}) collective-permute-start(bf16[96,768]{1,0:T(8,128)(2,1)S(1)} %get-tuple-element.138), channel_id=1, source_target_pairs={{0,16},{1,17},{2,18},{3,19},{4,20},{5,21},{6,22},{7,23},{8,24},{9,... | collective-permute-start | bytes 442376 | tf_op jit(solution)/shard_map/ppermute | solution.py:763
  342.9 17.5 %collective-permute-start.34 = (bf16[96,768]{1,0:T(8,128)(2,1)S(1)}, bf16[96,768]{1,0:T(8,128)(2,1)S(1)}, u32[]{:S(2)}, u32[]{:S(2)}) collective-permute-start(bf16[96,768]{1,0:T(8,128)(2,1)S(1)} %get-tuple-element.133), channel_id=1, source_target_pairs={{0,8},{1,9},{2,10},{3,11},{4,12},{5,13},{6,14},{7,15},{8,16},{9,17... | collective-permute-start | bytes 442376 | tf_op jit(solution)/shard_map/ppermute | solution.py:763
  344.2 20.0 %collective-permute-start.36 = (bf16[96,768]{1,0:T(8,128)(2,1)S(1)}, bf16[96,768]{1,0:T(8,128)(2,1)S(1)}, u32[]{:S(2)}, u32[]{:S(2)}) collective-permute-start(bf16[96,768]{1,0:T(8,128)(2,1)S(1)} %get-tuple-element.134), channel_id=1, source_target_pairs={{0,24},{1,25},{2,26},{3,27},{4,28},{5,29},{6,30},{7,31},{8,0},{9,1... | collective-permute-start | bytes 442376 | tf_op jit(solution)/shard_map/ppermute | solution.py:763
  353.8 11.5 %collective-permute-start.35 = (bf16[96,768]{1,0:T(8,128)(2,1)S(1)}, bf16[96,768]{1,0:T(8,128)(2,1)S(1)}, u32[]{:S(2)}, u32[]{:S(2)}) collective-permute-start(bf16[96,768]{1,0:T(8,128)(2,1)S(1)} %get-tuple-element.135), channel_id=1, source_target_pairs={{0,16},{1,17},{2,18},{3,19},{4,20},{5,21},{6,22},{7,23},{8,24},{9,... | collective-permute-start | bytes 442376 | tf_op jit(solution)/shard_map/ppermute | solution.py:763
  359.3 20.9 %collective-permute-start.20 = (bf16[512,768]{1,0:T(8,128)(2,1)}, bf16[512,768]{1,0:T(8,128)(2,1)S(1)}, u32[]{:S(2)}, u32[]{:S(2)}) collective-permute-start(bf16[512,768]{1,0:T(8,128)(2,1)} %fusion.18), channel_id=1, source_target_pairs={{0,2},{1,3},{2,0},{3,1},{4,6},{5,7},{6,4},{7,5},{8,10},{9,11},{10,... | collective-permute-start | bytes 2359304 | tf_op jit(solution)/shard_map/ppermute | solution.py:763
  360.3 9.7 %collective-permute-start.24 = (bf16[96,768]{0,1:T(8,128)(2,1)S(1)}, bf16[96,768]{0,1:T(8,128)(2,1)S(1)}, u32[]{:S(2)}, u32[]{:S(2)}) collective-permute-start(bf16[96,768]{0,1:T(8,128)(2,1)S(1)} %get-tuple-element.130), channel_id=1, source_target_pairs={{0,8},{1,9},{2,10},{3,11},{4,12},{5,13},{6,14},{7,15},{8,16},{9,17... | collective-permute-start | bytes 442376 | tf_op jit(solution)/shard_map/ppermute | solution.py:763
  360.4 9.7 %collective-permute-start.26 = (bf16[96,768]{0,1:T(8,128)(2,1)S(1)}, bf16[96,768]{0,1:T(8,128)(2,1)S(1)}, u32[]{:S(2)}, u32[]{:S(2)}) collective-permute-start(bf16[96,768]{0,1:T(8,128)(2,1)S(1)} %get-tuple-element.131), channel_id=1, source_target_pairs={{0,24},{1,25},{2,26},{3,27},{4,28},{5,29},{6,30},{7,31},{8,0},{9,1... | collective-permute-start | bytes 442376 | tf_op jit(solution)/shard_map/ppermute | solution.py:763
  364.2 14.2 %collective-permute-start.25 = (bf16[96,768]{0,1:T(8,128)(2,1)S(1)}, bf16[96,768]{0,1:T(8,128)(2,1)S(1)}, u32[]{:S(2)}, u32[]{:S(2)}) collective-permute-start(bf16[96,768]{0,1:T(8,128)(2,1)S(1)} %get-tuple-element.132), channel_id=1, source_target_pairs={{0,16},{1,17},{2,18},{3,19},{4,20},{5,21},{6,22},{7,23},{8,24},{9,... | collective-permute-start | bytes 442376 | tf_op jit(solution)/shard_map/ppermute | solution.py:763
  367.0 13.1 %copy-start.23 = (f32[768]{0:T(1024)S(1)}, f32[768]{0:T(1024)}, u32[]{:S(2)}) copy-start(f32[768]{0:T(1024)} %mul.64) | copy-start | bytes 9220
  367.0 13.1 %copy-start.25 = (f32[512]{0:T(512)S(1)}, f32[512]{0:T(512)}, u32[]{:S(2)}) copy-start(f32[512]{0:T(512)} %copy-done.24) | copy-start | bytes 6148
  367.0 13.1 %copy-start.26 = (f32[512]{0:T(512)S(1)}, f32[512]{0:T(512)}, u32[]{:S(2)}) copy-start(f32[512]{0:T(512)} %add_rsqrt_fusion) | copy-start | bytes 6148
  (19 other events, 85.0 us)
